TPU v7x, 32 devices: a whole 2x2x4 slice. The times are simulated.
32 devices in a mesh: grid: 8 (over z, y), bead: 4 (over x, core).
Axes of the slice: x: 2, y: 2, z: 4, core: 2. Of those that a mesh axis runs over, the one named last changes fastest.
Arguments:
- positions: float32 [3, 32, 4096], P(None, 'bead', 'grid'), may hold values from -6 to 6
- momenta: float32 [3, 32, 4096], P(None, 'bead', 'grid'), may hold values from -6 to 6
- noise: float32 [3, 32, 4096], P(None, 'bead', 'grid'), may hold values from -6 to 6
- charges: float32 [4096], P('grid'), may hold values from -5 to 5
- slab_route: int32 [4096, 1], P('grid'), may hold values from 0 to 7; in each aligned block of 512 rows (0 to 511, 512 to 1023, ...) at most 128 rows name the same one
- cells: int32 [3, 4096], P(None, 'grid'), may hold values from 0 to 255, as said below
- offsets: float32 [3, 4096], P(None, 'grid'), may hold values from 0 to 0.999
- nbr_tiles: int32 [32, 4], P('grid'), may hold values from 0 to 3
Outputs:
- new_positions: float32 [3, 32, 4096], P(None, 'bead', 'grid')
- new_momenta: float32 [3, 32, 4096], P(None, 'bead', 'grid')
Inputs may be any that keep to these rules, and one draw needn't show every extreme that they name: `slab_route`: among the 512 atoms of one domain at most 128 name the same slab, a bound that some block reaches of them. `cells`: row 0 lies below 32, row 1 below 256, row 2 below 256. `nbr_tiles`: tile numbers within the domain of the listing tile.
All inputs are finite; a program needn't handle non-finite values.
Results may differ from a plain program's by a relative error of at most 0.0003.
Values sent between devices are 32-bit elements; how exact they have to be, the bound alone decides.
A program may use at most 64 MiB of HBM per device.

v0:
```python
import functools
import math

import jax
import jax.numpy as jnp
import numpy as np
from jax import lax
from jax.experimental import pallas as pl
from jax.experimental.pallas import tpu as pltpu
from jax.sharding import PartitionSpec as P

GX = 256
GY = 256
GZ = 256
BEADS = 32
TILE = 128
NBR = 4


highest = lax.Precision.HIGHEST
time_step = 0.5
polymer_frequency = 1.0
centroid_friction = 0.5
coulomb_scale = 100000.0
screen_width = 200.0
pair_strength = 1.0 / 128.0
pair_range = 4.0


def spline(fraction):
    remain = 1.0 - fraction
    square = fraction * fraction
    cubic = square * fraction
    values = [
        remain * remain * remain / 6.0,
        (3.0 * cubic - 6.0 * square + 4.0) / 6.0,
        (-3.0 * cubic + 3.0 * square + 3.0 * fraction + 1.0) / 6.0,
        cubic / 6.0,
    ]
    slopes = [
        -0.5 * remain * remain,
        0.5 * (3.0 * square - 4.0 * fraction),
        0.5 * (-3.0 * square + 2.0 * fraction + 1.0),
        0.5 * square,
    ]
    return (values, slopes)


def pair_kernel(counts, places, momenta, kicked):
    beads, atoms = places.shape[1:]
    tiles = atoms // TILE
    across = [places[c].T for c in range(3)]

    def body(t, carry):
        where = pl.ds(pl.multiple_of(t * TILE, TILE), TILE)
        for b in range(beads):
            centre = [places[c, b : b + 1, where] for c in range(3)]
            sums = [jnp.zeros((8, TILE), jnp.float32) for _ in range(3)]
            for m in range(tiles):
                apart = [
                    centre[c] - across[c][m * TILE : (m + 1) * TILE, b : b + 1] for c in range(3)
                ]
                square = apart[0] * apart[0] + apart[1] * apart[1] + apart[2] * apart[2]
                weight = jnp.exp(square * (-1.0 / pair_range))
                for c in range(3):
                    part = jnp.sum((weight * apart[c]).reshape(TILE // 8, 8, TILE), axis=0)
                    sums[c] = sums[c] + counts[t, m] * part
            for c in range(3):
                force = jnp.sum(sums[c], axis=0, keepdims=True)
                kicked[c, b : b + 1, where] = momenta[c, b : b + 1, where] + force
        return carry

    lax.fori_loop(0, tiles, body, 0)


def kick_short(positions, momenta, neighbours):
    tiles = neighbours.shape[0]
    listed = neighbours[:, :, None] == jnp.arange(tiles, dtype=jnp.int32)
    counts = jnp.sum(listed.astype(jnp.float32), axis=1) * (0.5 * time_step * pair_strength)
    pairs = positions.shape[1] * positions.shape[2] ** 2
    vmem = pl.BlockSpec(memory_space=pltpu.VMEM)
    return pl.pallas_call(
        pair_kernel,
        out_shape=jax.ShapeDtypeStruct(momenta.shape, jnp.float32),
        in_specs=[pl.BlockSpec(memory_space=pltpu.SMEM), vmem, vmem],
        out_specs=vmem,
        cost_estimate=pl.CostEstimate(
            flops=20 * pairs, bytes_accessed=12 * positions.size, transcendentals=pairs
        ),
    )(counts, positions, momenta)


def grid_positions(target, cells, offsets, planes):
    first = (target * planes + cells[0]).astype(jnp.float32) + offsets[0]
    second = cells[1].astype(jnp.float32) + offsets[1]
    third = cells[2].astype(jnp.float32) + offsets[2]
    return jnp.stack([first, second, third])


def real_waves(length):
    half = length // 2
    row = np.arange(length)
    wave = np.where(row <= half, row, row - half)
    angle = (wave[:, None] * np.arange(length)[None, :] % length) * (2.0 * math.pi / length)
    table = np.where((row <= half)[:, None], np.cos(angle), np.sin(angle))
    count = np.where((wave == 0) | (wave == half), 1.0, 2.0)
    return table, wave, count


def split_table(table):
    high = table.astype(jnp.bfloat16)
    low = (table - high.astype(np.float64)).astype(jnp.bfloat16)
    return high, low


def split(value):
    high = value.astype(jnp.bfloat16)
    low = (value - high.astype(jnp.float32)).astype(jnp.bfloat16)
    return high, low


def dot3(left, right, dims):
    def one(a, b):
        return lax.dot_general(a, b, (dims, ((), ())), preferred_element_type=jnp.float32)

    return one(left[0], right[0]) + (one(left[0], right[1]) + one(left[1], right[0]))


def stencil(position, length, with_slope):
    lowest = jnp.floor(position)
    values, slopes = spline(position - lowest)
    cell = lax.broadcasted_iota(jnp.int32, (length, position.shape[1]), 0)
    step = (cell - (lowest.astype(jnp.int32) - 1)) & (length - 1)
    step = step.astype(jnp.int16)
    hits = [step == jnp.asarray(offset, step.dtype) for offset in range(4)]

    def dense(members):
        out = jnp.zeros(step.shape, jnp.bfloat16)
        for offset in range(4):
            out = jnp.where(hits[offset], members[offset], out)
        return out

    def both(members):
        halves = [split(member) for member in members]
        return dense([half[0] for half in halves]), dense([half[1] for half in halves])

    return (both(values), both(slopes)) if with_slope else (both(values),)


def mesh_kernel(chunks, group, fields, rxh, rxl, ryh, ryl, rzh, rzl, screen, out, total, gh, gl, xs, xd):
    step = pl.program_id(0)
    nx = rxh.shape[0]
    ny = ryh.shape[0]
    atoms = fields.shape[1]
    rows = group * ny
    nn = ((1,), (0,))
    nt = ((1,), (1,))

    def along(high, low, dense):
        return dot3((high[...], low[...]), dense, nn)

    @pl.when(step == 0)
    def _():
        total[...] = jnp.zeros_like(total)

    @pl.when(step < chunks)
    def _():
        xs[...] = along(rxh, rxl, stencil(fields[1:2, :], GX, False)[0]) * fields[0:1, :]
        ys = along(ryh, ryl, stencil(fields[2:3, :], GY, False)[0])
        zs = split(along(rzh, rzl, stencil(fields[3:4, :], GZ, False)[0]))

        def body(index, carry):
            parts = [xs[pl.ds(index * group + j, 1), :] * ys for j in range(group)]
            pair = split(jnp.concatenate(parts, axis=0))
            where = pl.ds(pl.multiple_of(index * rows, rows), rows)
            total[where, :] += dot3(pair, zs, nt)
            return carry

        lax.fori_loop(0, nx // group, body, 0, unroll=True)

    @pl.when(step == chunks - 1)
    def _():
        def body(index, carry):
            where = pl.ds(pl.multiple_of(index * rows, rows), rows)
            high, low = split(total[where, :] * screen[where, :])
            gh[where, :] = high
            gl[where, :] = low
            return carry

        lax.fori_loop(0, nx // group, body, 0)

    @pl.when(step >= chunks)
    def _():
        value, slope = stencil(fields[1:2, :], GX, True)
        xs[...] = along(rxh, rxl, value)
        xd[...] = along(rxh, rxl, slope)
        value, slope = stencil(fields[2:3, :], GY, True)
        ys = along(ryh, ryl, value)
        yd = along(ryh, ryl, slope)
        value, slope = stencil(fields[3:4, :], GZ, True)
        zs = split(along(rzh, rzl, value))
        zd = split(along(rzh, rzl, slope))

        def body(index, carry):
            force_x, force_y, force_z = carry
            where = pl.ds(pl.multiple_of(index * rows, rows), rows)
            filtered = (gh[where, :], gl[where, :])
            plain = dot3(filtered, zs, nn)
            steep = dot3(filtered, zd, nn)
            for j in range(group):
                own = plain[j * ny : (j + 1) * ny]
                x_here = xs[pl.ds(index * group + j, 1), :]
                force_x += xd[pl.ds(index * group + j, 1), :] * jnp.sum(own * ys, axis=0, keepdims=True)
                force_y += x_here * jnp.sum(own * yd, axis=0, keepdims=True)
                force_z += x_here * jnp.sum(
                    steep[j * ny : (j + 1) * ny] * ys, axis=0, keepdims=True
                )
            return force_x, force_y, force_z

        empty = jnp.zeros((1, atoms), jnp.float32)
        found = lax.fori_loop(0, nx // group, body, (empty, empty, empty), unroll=True)
        for c in range(3):
            out[c : c + 1, :] = -fields[0:1, :] * found[c]


def mesh_forces(fields, row_x, row_y, nx, ny):
    table_x, wave_x, count_x = real_waves(GX)
    table_y, wave_y, count_y = real_waves(GY)
    table_z, wave_z, count_z = real_waves(GZ)

    def rows_of(values, first, count):
        return lax.dynamic_slice_in_dim(jnp.asarray(values), first, count, 0)

    own = [rows_of(part, row_x, nx) for part in split_table(table_x)]
    own += [rows_of(part, row_y, ny) for part in split_table(table_y)]
    own += [jnp.asarray(part) for part in split_table(table_z)]
    square_x = rows_of((wave_x**2).astype(np.float32), row_x, nx)
    square_y = rows_of((wave_y**2).astype(np.float32), row_y, ny)
    times_x = rows_of((count_x / float(GX)).astype(np.float32), row_x, nx)
    times_y = rows_of((count_y / float(GY)).astype(np.float32), row_y, ny)
    square_z = jnp.asarray((wave_z**2).astype(np.float32))
    times_z = jnp.asarray((count_z / float(GZ)).astype(np.float32))
    square = (square_x[:, None] + square_y[None, :]).reshape(nx * ny, 1) + square_z[None, :]
    times = (times_x[:, None] * times_y[None, :]).reshape(nx * ny, 1) * times_z[None, :]
    centre = square == 0.0
    screen = jnp.where(
        centre,
        0.0,
        coulomb_scale
        * jnp.exp(-square / (2.0 * screen_width * screen_width))
        / jnp.where(centre, 1.0, square),
    )
    screen = screen * times

    atoms = fields.shape[1]
    width = min(512, atoms)
    chunks = atoms // width
    group = min(8, nx)
    full = lambda array: pl.BlockSpec(array.shape, lambda s: (0, 0))
    operands = [fields, *own, screen]
    return pl.pallas_call(
        functools.partial(mesh_kernel, chunks, group),
        grid=(2 * chunks,),
        out_shape=jax.ShapeDtypeStruct((3, atoms), jnp.float32),
        in_specs=[pl.BlockSpec((4, width), lambda s: (0, s % chunks))]
        + [full(array) for array in operands[1:]],
        out_specs=pl.BlockSpec((3, width), lambda s: (0, jnp.maximum(s - chunks, 0))),
        scratch_shapes=[
            pltpu.VMEM((nx * ny, GZ), jnp.float32),
            pltpu.VMEM((nx * ny, GZ), jnp.bfloat16),
            pltpu.VMEM((nx * ny, GZ), jnp.bfloat16),
            pltpu.VMEM((nx, width), jnp.float32),
            pltpu.VMEM((nx, width), jnp.float32),
        ],
        compiler_params=pltpu.CompilerParams(
            dimension_semantics=("arbitrary",), vmem_limit_bytes=48 * 1024 * 1024
        ),
        cost_estimate=pl.CostEstimate(
            flops=18 * nx * ny * GZ * atoms, bytes_accessed=8 * nx * ny * GZ, transcendentals=0
        ),
    )(*operands)


def step_tables(bead_total):
    mode = np.arange(bead_total)
    angle = (mode[:, None] * mode[None, :] % bead_total) * (2.0 * math.pi / bead_total)
    middle = bead_total // 2
    scaled = math.sqrt(2.0 / bead_total)
    column = mode[:, None]
    matrix = np.where(
        column == 0,
        1.0 / math.sqrt(bead_total),
        np.where(
            column < middle,
            scaled * np.cos(angle),
            np.where(
                column == middle, np.cos(angle) / math.sqrt(bead_total), scaled * np.sin(angle)
            ),
        ),
    )
    half = 0.5 * time_step
    frequency = 2.0 * polymer_frequency * np.sin(mode * (math.pi / bead_total))
    cosine = np.cos(frequency * half)
    drift = np.where(mode == 0, half, np.sin(frequency * half) / np.where(mode == 0, 1.0, frequency))
    pull = frequency * np.sin(frequency * half)
    friction = np.where(mode == 0, centroid_friction, 2.0 * frequency)
    damping = np.exp(-friction * time_step)
    kick = np.sqrt(1.0 - damping * damping)
    factors = [
        [cosine * cosine - drift * damping * pull, drift * cosine * (1.0 + damping), drift * kick],
        [-cosine * pull * (1.0 + damping), cosine * damping * cosine - pull * drift, cosine * kick],
    ]
    tables = np.stack(
        [
            np.stack(
                [
                    matrix.T @ (row[0][:, None] * matrix),
                    matrix.T @ (row[1][:, None] * matrix),
                    matrix.T * row[2][None, :],
                ]
            )
            for row in factors
        ]
    )
    return tables.astype(np.float32), (float(factors[0][1][0]), float(factors[1][1][0]))


def per_device(positions, momenta, noise, charges, slab_route, cells, offsets, nbr_tiles):
    grid_count = lax.axis_size("grid")
    bead_count = lax.axis_size("bead")
    grid_rank = lax.axis_index("grid")
    bead_rank = lax.axis_index("bead")
    beads_local = positions.shape[1]
    nx = GX // grid_count
    ny = GY // bead_count
    half_step = 0.5 * time_step

    grid_pos = grid_positions(slab_route[:, 0], cells, offsets, nx)
    fields = jnp.concatenate([charges[None, :], grid_pos], axis=0)
    copies = jnp.broadcast_to(fields[:, None, :], (4, grid_count, charges.shape[0]))
    fields = lax.all_to_all(copies, "grid", split_axis=1, concat_axis=1, tiled=True)
    fields = fields.reshape(4, grid_count * charges.shape[0])
    partial = mesh_forces(fields, grid_rank * nx, bead_rank * ny, nx, ny)
    shares = lax.all_to_all(
        partial.reshape(3, grid_count, charges.shape[0]), "grid", split_axis=1, concat_axis=1, tiled=True
    )
    mesh_force = half_step * lax.psum(jnp.sum(shares, axis=1), "bead")

    kicked = kick_short(positions, momenta, nbr_tiles)
    sources = lax.all_gather(
        jnp.stack([positions, kicked, noise]), "bead", axis=2, tiled=True
    )
    tables, (centre_q, centre_p) = step_tables(beads_local * bead_count)
    own = lax.dynamic_slice_in_dim(jnp.asarray(tables), bead_rank * beads_local, beads_local, 2)
    stepped = jnp.einsum("okbm,kcma->ocba", own, sources, precision=highest)
    return (
        stepped[0] + centre_q * mesh_force[:, None, :],
        stepped[1] + centre_p * mesh_force[:, None, :],
    )


def solution(mesh):
    in_specs = (
        P(None, "bead", "grid"),
        P(None, "bead", "grid"),
        P(None, "bead", "grid"),
        P("grid"),
        P("grid", None),
        P(None, "grid"),
        P(None, "grid"),
        P("grid", None),
    )
    out_specs = (P(None, "bead", "grid"), P(None, "bead", "grid"))
    return jax.shard_map(
        per_device, mesh=mesh, in_specs=in_specs, out_specs=out_specs, check_vma=False
    )
```

profile of v0, /device:TPU:0, one launch (start us, length us, event | category | flops | bytes accessed | tf_op | source)
XLA Modules:
  0.0 117.7 jit_solution(10859071334905215259)
XLA Ops:
  0.6 0.8 fusion.12
  1.5 0.7 pad_maximum_fusion.1
  2.2 0.6 broadcast_in_dim.9
  2.8 0.0 copy-start.2
  2.8 7.4 %all-to-all-start = ((f32[4,8,512]{2,0,1:T(4,128)}), f32[4,8,512]{2,0,1:T(4,128)S(1)}, u32[]{:S(2)}, u32[]{:S(2)}) async-start(f32[4,8,512]{2,0,1:T(4,128)} %broadcast_in_dim.9), calls=%async_computation | async-start | bytes 131072 | tf_op jit(solution)/shard_map/all_to_all | solution.py:341
  10.2 0.8 dynamic_slice.33
  11.0 0.8 dynamic_slice.32
  11.7 0.8 dynamic_slice.35
  12.5 0.8 dynamic_slice.34
  13.2 0.1 broadcast_add_fusion
  13.3 0.1 add.92
  13.4 0.1 broadcast_multiply_fusion
  13.4 0.1 mul.98
  13.5 0.8 convert_reduce_fusion
  14.3 0.6 broadcast_multiply_fusion.3.counts
  14.9 8.7 %shard_map.212 = f32[3,8,512]{2,1,0:T(8,128)} custom-call(f32[4,4]{1,0:T(4,128)} %broadcast_multiply_fusion.3.counts, f32[3,8,512]{2,1,0:T(8,128)} %places.1, f32[3,8,512]{2,1,0:T(8,128)} %momenta.1), custom_call_target="tpu_custom_call" | custom-call | flops 41943040 | bytes 147456 | tf_op jit(solution)/shard_map/pallas_call | solution.py:82
  23.5 0.0 copy-done.2
  23.6 0.0 copy-done.3
  23.6 0.9 pad_maximum_fusion
  24.4 7.5 %all_gather.3 = f32[3,3,32,512]{3,2,1,0:T(8,128)S(1)} all-gather(f32[3,3,8,512]{3,2,1,0:T(8,128)S(1)} %pad_maximum_fusion), channel_id=1, replica_groups=mesh['grid'=8,'bead'=4] {'bead'}, dimensions={2}, use_global_device_ids=true | all-gather | bytes 737280 | tf_op jit(solution)/shard_map/all_gather | solution.py:350
  31.9 0.0 copy-done.4
  32.0 0.0 copy-done.5
  32.0 0.9 fusion.1.screen
  32.8 0.0 copy-done
  32.9 0.0 copy-done.1
  32.9 0.0 all-to-all-done
  32.9 65.1 %shard_map.213 = f32[3,4096]{1,0:T(4,128)} custom-call(f32[4,4096]{1,0:T(4,128)S(1)} %bitcast.32, bf16[32,256]{1,0:T(8,128)(2,1)S(1)} %get-tuple-element.10.rxh, bf16[32,256]{1,0:T(8,128)(2,1)S(1)} %get-tuple-element.9.rxl, bf16[64,256]{1,0:T(8,128)(2,1)S(1)} %get-tuple-element.12.ryh, bf16[64,256]{1,0:T(8,128)(2,1)S(1)} %get-tuple-element.11.ryl, ...), custom_call_target="tpu_custom_call" | custom-call | flops 38654705664 | bytes 4194304 | tf_op jit(solution)/shard_map/pallas_call | solution.py:261
  98.0 6.0 %all-to-all-start.1 = ((f32[3,8,512]{2,0,1:T(4,128)}), f32[3,8,512]{2,0,1:T(4,128)S(1)}, u32[]{:S(2)}, u32[]{:S(2)}) async-start(f32[3,8,512]{2,0,1:T(4,128)} %bitcast.12), calls=%async_computation.1 | async-start | bytes 131072 | tf_op jit(solution)/shard_map/all_to_all | solution.py:344
  104.0 1.2 convolution_bitcast_fusion
  105.2 5.7 %all-to-all-done.1 = f32[3,8,512]{2,0,1:T(4,128)S(1)} async-done(((f32[3,8,512]{2,0,1:T(4,128)}), f32[3,8,512]{2,0,1:T(4,128)S(1)}, u32[]{:S(2)}, u32[]{:S(2)}) %all-to-all-start.1) | async-done | bytes 49184 | tf_op jit(solution)/shard_map/all_to_all | solution.py:344
  110.9 6.1 %psum.7 = f32[3,512]{1,0:T(4,128)S(1)} all-reduce(f32[3,512]{1,0:T(4,128)S(1)} %reduce_sum.19), channel_id=1, replica_groups=mesh['grid'=8,'bead'=4] {'bead'}, use_global_device_ids=true, to_apply=%region_2.3 | all-reduce | flops 1536 | bytes 12288 | tf_op jit(solution)/shard_map/psum | solution.py:347
  117.0 0.6 fusion.7
  (9 shorter events, 0.1 us)
Async XLA Ops:
  2.8 20.7 %copy-start.2 = (f32[3,8,512]{2,1,0:T(8,128)S(1)}, f32[3,8,512]{2,1,0:T(8,128)}, u32[]{:S(2)}) copy-start(f32[3,8,512]{2,1,0:T(8,128)} %param.23) | copy-start | bytes 147460
  2.8 20.8 %copy-start.3 = (f32[3,8,512]{2,1,0:T(8,128)S(1)}, f32[3,8,512]{2,1,0:T(8,128)}, u32[]{:S(2)}) copy-start(f32[3,8,512]{2,1,0:T(8,128)} %places.1) | copy-start | bytes 147460
  2.8 30.1 %all-to-all-start = ((f32[4,8,512]{2,0,1:T(4,128)}), f32[4,8,512]{2,0,1:T(4,128)S(1)}, u32[]{:S(2)}, u32[]{:S(2)}) async-start(f32[4,8,512]{2,0,1:T(4,128)} %broadcast_in_dim.9), calls=%async_computation | async-start | bytes 131072 | tf_op jit(solution)/shard_map/all_to_all | solution.py:341
  14.9 17.1 %copy-start.4 = (f32[256]{0:T(256)S(1)}, f32[256]{0:T(256)}, u32[]{:S(2)}) copy-start(f32[256]{0:T(256)} %constant.51.clone) | copy-start | bytes 3076
  14.9 17.1 %copy-start.5 = (f32[256]{0:T(256)S(1)}, f32[256]{0:T(256)}, u32[]{:S(2)}) copy-start(f32[256]{0:T(256)} %constant.52.clone) | copy-start | bytes 3076
  23.5 9.3 %copy-start = (bf16[256,256]{1,0:T(8,128)(2,1)S(1)}, bf16[256,256]{1,0:T(8,128)(2,1)}, u32[]{:S(2)}) copy-start(bf16[256,256]{1,0:T(8,128)(2,1)} %constant.49.clone.rzh) | copy-start | bytes 393220
  23.5 9.3 %copy-start.1 = (bf16[256,256]{1,0:T(8,128)(2,1)S(1)}, bf16[256,256]{1,0:T(8,128)(2,1)}, u32[]{:S(2)}) copy-start(bf16[256,256]{1,0:T(8,128)(2,1)} %constant.50.clone.rzl) | copy-start | bytes 393220
  98.0 12.9 %all-to-all-start.1 = ((f32[3,8,512]{2,0,1:T(4,128)}), f32[3,8,512]{2,0,1:T(4,128)S(1)}, u32[]{:S(2)}, u32[]{:S(2)}) async-start(f32[3,8,512]{2,0,1:T(4,128)} %bitcast.12), calls=%async_computation.1 | async-start | bytes 131072 | tf_op jit(solution)/shard_map/all_to_all | solution.py:344
where the time goes:
time: 118 us
  Pallas kernels  73.8 us (63%)
  blocking collectives  13.6 us (12%)
  starting transfers between devices  13.4 us (11%)
  waiting for transfers between devices  5.74 us (5%)
  other arithmetic  5.44 us (5%)
  local copies, waits for them, and re-layouts  3.84 us (3%)
    pallas_call x1, Pallas kernels, mesh_forces(): pl.pallas_call(functools.partial(mesh_kernel, chunks, group), grid=(2 * c...  65.1 us
    pallas_call x1, Pallas kernels, kick_short(): pl.pallas_call(pair_kernel, out_shape=jax.ShapeDtypeStruct(momenta.shape,...  8.67 us
    all_gather x1, blocking collectives, per_device(): lax.all_gather(jnp.stack([positions, kicked, noise]), 'bead', axis=2, til...  7.53 us
    all_to_all x1, starting transfers between devices, per_device(): lax.all_to_all(copies, 'grid', split_axis=1, concat_axis=1, tiled=True)  7.41 us
    psum x1, blocking collectives, per_device(): mesh_force = half_step * lax.psum(jnp.sum(shares, axis=1), 'bead')  6.07 us
    all_to_all x1, starting transfers between devices, per_device(): lax.all_to_all(partial.reshape(3, grid_count, charges.shape[0]), 'grid',...  6 us
    all_to_all x1, waiting for transfers between devices, per_device(): lax.all_to_all(partial.reshape(3, grid_count, charges.shape[0]), 'grid',...  5.74 us
    dynamic_slice x6, local copies, waits for them, and re-layouts, rows_of(): return lax.dynamic_slice_in_dim(jnp.asarray(values), first, count, 0)  3.03 us
  transfers between devices with their start and end apart: 2, of which 1 were waited for; matrix products, arithmetic and copies ran while one was open for 6% of the time, Pallas kernels for 7%

commit v1 on v0

v1 whole, which is shorter than its diff:
```python
import functools
import math

import jax
import jax.numpy as jnp
import numpy as np
from jax import lax
from jax.experimental import pallas as pl
from jax.experimental.pallas import tpu as pltpu
from jax.sharding import PartitionSpec as P

GX = GY = GZ = 256
WAVES = 8
BIN = 32
WINDOW = 40
CAP = 128
coulomb_scale = 100000.0
screen_width = 200.0

def spline(fraction):
    remain = 1.0 - fraction
    square = fraction * fraction
    cubic = square * fraction
    values = [
        remain * remain * remain / 6.0,
        (3.0 * cubic - 6.0 * square + 4.0) / 6.0,
        (-3.0 * cubic + 3.0 * square + 3.0 * fraction + 1.0) / 6.0,
        cubic / 6.0,
    ]
    slopes = [
        -0.5 * remain * remain,
        0.5 * (3.0 * square - 4.0 * fraction),
        0.5 * (-3.0 * square + 2.0 * fraction + 1.0),
        0.5 * square,
    ]
    return (values, slopes)

def real_waves(length):
    half = length // 2
    row = np.arange(length)
    wave = np.where(row <= half, row, row - half)
    angle = (wave[:, None] * np.arange(length)[None, :] % length) * (2.0 * math.pi / length)
    return np.where((row <= half)[:, None], np.cos(angle), np.sin(angle))

def split_table(table):
    high = table.astype(jnp.bfloat16)
    low = (table - high.astype(np.float64)).astype(jnp.bfloat16)
    return high, low

def split(value):
    high = value.astype(jnp.bfloat16)
    low = (value - high.astype(jnp.float32)).astype(jnp.bfloat16)
    return high, low

NN = ((1,), (0,))
NT = ((1,), (1,))

def dot3(left, right, dims):
    def one(a, b):
        return lax.dot_general(a, b, (dims, ((), ())), preferred_element_type=jnp.float32)
    return one(left[0], right[0]) + (one(left[0], right[1]) + one(left[1], right[0]))

def stencil(position, length, with_slope):
    lowest = jnp.floor(position)
    values, slopes = spline(position - lowest)
    cell = lax.broadcasted_iota(jnp.int32, (length, position.shape[1]), 0)
    step = (cell - (lowest.astype(jnp.int32) - 1)) & (length - 1)
    step = step.astype(jnp.int16)
    hits = [step == jnp.asarray(offset, step.dtype) for offset in range(4)]

    def dense(members):
        out = jnp.zeros(step.shape, jnp.bfloat16)
        for offset in range(4):
            out = jnp.where(hits[offset], members[offset], out)
        return out

    def both(members):
        halves = [split(member) for member in members]
        return dense([half[0] for half in halves]), dense([half[1] for half in halves])

    return (both(values), both(slopes)) if with_slope else (both(values),)

def window(position, base, with_slope):
    lowest = jnp.floor(position)
    values, slopes = spline(position - lowest)
    cell = lax.broadcasted_iota(jnp.int32, (WINDOW, position.shape[1]), 0)
    step = cell - (lowest.astype(jnp.int32) - base)
    hits = [step == offset for offset in range(4)]

    def dense(members):
        out = jnp.zeros(step.shape, jnp.float32)
        for offset in range(4):
            out = jnp.where(hits[offset], members[offset], out)
        return out

    return (dense(values), dense(slopes)) if with_slope else (dense(values),)

def wave_of(group, shape):
    row = lax.broadcasted_iota(jnp.int32, shape, 0)
    half = WAVES // 2
    odd = (group == 0) & (row == half)
    wave = jnp.where(odd, GY // 2, group * half + (row & (half - 1)))
    turn = jnp.where((row < half) | odd, 0, -(GY // 4))
    return wave, turn

def turned(phase):
    phase = phase & (GY - 1)
    angle = (GY // 4 - jnp.abs(phase - GY // 2)).astype(jnp.float32) * (2.0 * math.pi / GY)
    square = angle * angle
    total = 1.0 / 6227020800.0
    for power in (39916800.0, 362880.0, 5040.0, 120.0, 6.0, 1.0):
        sign = -1.0 if power in (39916800.0, 5040.0, 6.0) else 1.0
        total = total * square + sign / power
    return -(angle * total)

def lines(position, group, with_slope):
    lowest = jnp.floor(position)
    values, slopes = spline(position - lowest)
    wave, turn = wave_of(group, (WAVES, position.shape[1]))
    phase = wave * (lowest.astype(jnp.int32) - 1) + turn
    value = slope = 0.0
    for offset in range(4):
        cosine = turned(phase)
        value = value + values[offset] * cosine
        if with_slope:
            slope = slope + slopes[offset] * cosine
        phase = phase + wave
    return (value, slope) if with_slope else (value,)

def mesh_kernel(axes, fields, fxh, fxl, fxth, fxtl, rh, rl, rth, rtl, out, total, filt, wave2):
    domains = fields.shape[0]
    grid_name, bead_name = axes
    bead_count = lax.axis_size(bead_name)
    device = lax.axis_index(grid_name) * bead_count + lax.axis_index(bead_name)
    groups = GY // WAVES
    parts = lax.axis_size(grid_name) * bead_count // groups
    group = lax.rem(device, groups)
    part = lax.div(device, groups)
    bins = GX // BIN
    pack = min(2, domains)
    unroll = min(8, domains) // pack
    chunks = domains // (pack * unroll)

    def block(first, where):
        own = [fields[first + i, :, where] for i in range(pack)]
        return jnp.concatenate(own, axis=1)

    row = lax.broadcasted_iota(jnp.int32, (GX, GZ), 0)
    col = lax.broadcasted_iota(jnp.int32, (GX, GZ), 1)
    wx = jnp.where(row <= GX // 2, row, row - GX // 2)
    wz = jnp.where(col <= GZ // 2, col, col - GZ // 2)
    square = (wx * wx + wz * wz).astype(jnp.float32)
    times = jnp.where((wx & (GX // 2 - 1)) == 0, 1.0, 2.0) * jnp.where((wz & (GZ // 2 - 1)) == 0, 1.0, 2.0)
    if parts > 1:
        times = jnp.where(lax.div(col * parts, GZ) == part, times, 0.0)
    wave2[...] = square
    filt[...] = times * jnp.exp(square * (-1.0 / (2.0 * screen_width * screen_width)))

    for r in range(WAVES):
        total[r, 0:GX + 8, :] = jnp.zeros((GX + 8, GZ), jnp.float32)

    def spread(step, carry):
        s = step // chunks
        where = pl.ds(pl.multiple_of(s * CAP, CAP), CAP)
        base = s * BIN
        part_sum = None
        for j in range(unroll):
            own = block((step % chunks) * (unroll * pack) + j * pack, where)
            x, = window(own[1:2], base, False)
            y, = lines(own[2:3], group, False)
            z, = stencil(own[3:4], GZ, False)
            y = y * own[0:1]
            rows = split(jnp.concatenate([x * y[r:r + 1] for r in range(WAVES)], axis=0))
            got = dot3(rows, z, NT)
            part_sum = got if part_sum is None else part_sum + got
        rows = pl.ds(pl.multiple_of(base, 8), WINDOW)
        for r in range(WAVES):
            total[r, rows, :] += part_sum[r * WINDOW:(r + 1) * WINDOW]
        return carry
    lax.fori_loop(0, bins * chunks, spread, 0)

    def transform(r, carry):
        wave, _ = wave_of_row(group, r)
        wave = jnp.full((1, GZ), wave, jnp.int32)
        wave_square = (wave * wave).astype(jnp.float32)
        count = jnp.where((wave & (GY // 2 - 1)) == 0, 1.0, 2.0)
        scale = count * jnp.exp(wave_square * (-1.0 / (2.0 * screen_width * screen_width))) * (coulomb_scale / (GX * GY * GZ))
        total[r, 0:8, :] += total[r, GX:GX + 8, :]
        t = dot3((fxh[...], fxl[...]), split(total[r, 0:GX, :]), NN)
        t = dot3(split(t), (rth[...], rtl[...]), NN)
        m2 = wave2[...] + wave_square
        t = t * jnp.where(m2 == 0.0, 0.0, filt[...] * scale / jnp.where(m2 == 0.0, 1.0, m2))
        t = dot3(split(t), (rh[...], rl[...]), NN)
        t = dot3((fxth[...], fxtl[...]), split(t), NN)
        total[r, 0:GX, :] = t
        total[r, GX:GX + 8, :] = t[0:8]
        return carry
    lax.fori_loop(0, WAVES, transform, 0)

    def gather(step, carry):
        s = step // chunks
        where = pl.ds(pl.multiple_of(s * CAP, CAP), CAP)
        base = s * BIN
        rows = pl.ds(pl.multiple_of(base, 8), WINDOW)
        near = split(jnp.concatenate([total[r, rows, :] for r in range(WAVES)], axis=0))
        for j in range(unroll):
            first = (step % chunks) * (unroll * pack) + j * pack
            own = block(first, where)
            x, xd = window(own[1:2], base, True)
            y, yd = lines(own[2:3], group, True)
            z, zd = stencil(own[3:4], GZ, True)
            plain = dot3(near, z, NN)
            steep = dot3(near, zd, NN)
            f = [0.0, 0.0, 0.0]
            for r in range(WAVES):
                q = plain[r * WINDOW:(r + 1) * WINDOW]
                f[0] = f[0] + q * y[r:r + 1]
                f[1] = f[1] + q * yd[r:r + 1]
                f[2] = f[2] + steep[r * WINDOW:(r + 1) * WINDOW] * y[r:r + 1]
            f = [f[0] * xd, f[1] * x, f[2] * x]
            for c in range(3):
                force = -own[0:1] * jnp.sum(f[c], axis=0, keepdims=True)
                for i in range(pack):
                    out[first + i, c:c + 1, where] = force[:, i * CAP:(i + 1) * CAP]
        return carry
    lax.fori_loop(0, bins * chunks, gather, 0)

def wave_of_row(group, row):
    half = WAVES // 2
    odd = (group == 0) & (row == half)
    wave = jnp.where(odd, GY // 2, group * half + (row & (half - 1)))
    return wave, odd

def mesh_forces(fields, axes=("grid", "bead")):
    domains = fields.shape[0]
    table = real_waves(GX)
    shifted = np.roll(table, 1, axis=1)
    tables = []
    for t in (shifted, shifted.T, table, table.T):
        tables += [jnp.asarray(v) for v in split_table(t)]
    vmem = pl.BlockSpec(memory_space=pltpu.VMEM)
    return pl.pallas_call(
        functools.partial(mesh_kernel, axes),
        out_shape=jax.ShapeDtypeStruct((domains, 3, GX // BIN * CAP), jnp.float32),
        in_specs=[vmem] * 9,
        out_specs=vmem,
        scratch_shapes=[
            pltpu.VMEM((WAVES, GX + 8, GZ), jnp.float32),
            pltpu.VMEM((GX, GZ), jnp.float32),
            pltpu.VMEM((GX, GZ), jnp.float32),
        ],
        compiler_params=pltpu.CompilerParams(vmem_limit_bytes=48 * 1024 * 1024),
    )(fields, *tables)


TILE = 128
highest = lax.Precision.HIGHEST
time_step = 0.5
polymer_frequency = 1.0
centroid_friction = 0.5
pair_strength = 1.0 / 128.0
pair_range = 4.0
MESH = pl.DeviceIdType.MESH


def greet(names):
    barrier = pltpu.get_barrier_semaphore()
    total = 0
    for name in names:
        count = lax.axis_size(name)
        me = lax.axis_index(name)

        def signal(step, carry):
            peer = lax.rem(me + step, count)
            pl.semaphore_signal(barrier, 1, device_id={name: peer}, device_id_type=MESH)
            return carry

        lax.fori_loop(1, count, signal, 0)
        total += count - 1
    pl.semaphore_wait(barrier, total)


def shares(name, source, target, send_sem, recv_sem):
    count = lax.axis_size(name)
    me = lax.axis_index(name)

    def copy(step, landing):
        peer = lax.rem(me + step, count)
        return pltpu.make_async_remote_copy(
            src_ref=source(peer),
            dst_ref=target(peer if landing else me),
            send_sem=send_sem.at[peer],
            recv_sem=recv_sem.at[peer if landing else me],
            device_id={name: peer},
            device_id_type=MESH,
        )

    def start():
        def one(step, carry):
            copy(step, False).start()
            return carry

        lax.fori_loop(1, count, one, 0)

    def wait():
        def one(step, carry):
            copy(step, True).wait_recv()
            return carry

        lax.fori_loop(1, count, one, 0)

    def drain():
        def one(step, carry):
            copy(step, False).wait_send()
            return carry

        lax.fori_loop(1, count, one, 0)

    return start, wait, drain


def split3(value):
    high = value.astype(jnp.bfloat16)
    rest = value - high.astype(jnp.float32)
    middle = rest.astype(jnp.bfloat16)
    return high, middle, (rest - middle.astype(jnp.float32)).astype(jnp.bfloat16)


def slots_of(route, per_bin):
    atoms = route.shape[1]
    bins = GX // BIN
    owner = lax.div(route, per_bin)
    bin_row = lax.broadcasted_iota(jnp.int32, (2 * bins, atoms), 0)
    mine = bin_row == owner
    before = lax.broadcasted_iota(jnp.int32, (atoms, atoms), 0)
    after = lax.broadcasted_iota(jnp.int32, (atoms, atoms), 1)
    earlier = jnp.where(before < after, 1.0, 0.0).astype(jnp.bfloat16)
    chosen = jnp.where(mine, 1.0, 0.0)
    rank = jnp.dot(chosen.astype(jnp.bfloat16), earlier, preferred_element_type=jnp.float32)
    rank = jnp.sum(chosen * rank, axis=0, keepdims=True)
    return owner * CAP + rank.astype(jnp.int32)


def placement(slot):
    spots = lax.broadcasted_iota(jnp.int32, (GX // BIN * CAP, slot.shape[1]), 0)
    return jnp.where(spots == slot, 1.0, 0.0).astype(jnp.bfloat16)


def pair_forces(weight_of, positions, momenta, kicked):
    beads, atoms = positions.shape[1:]
    tiles = atoms // TILE
    across = [positions[c].T for c in range(3)]

    def body(t, carry):
        where = pl.ds(pl.multiple_of(t * TILE, TILE), TILE)
        for b in range(beads):
            centre = [positions[c, b : b + 1, where] for c in range(3)]
            sums = [jnp.zeros((8, TILE), jnp.float32) for _ in range(3)]
            for m in range(tiles):
                apart = [
                    centre[c] - across[c][m * TILE : (m + 1) * TILE, b : b + 1] for c in range(3)
                ]
                square = apart[0] * apart[0] + apart[1] * apart[1] + apart[2] * apart[2]
                weight = jnp.exp(square * (-1.0 / pair_range))
                for c in range(3):
                    part = jnp.sum((weight * apart[c]).reshape(TILE // 8, 8, TILE), axis=0)
                    sums[c] = sums[c] + weight_of(t, m) * part
            for c in range(3):
                force = jnp.sum(sums[c], axis=0, keepdims=True)
                kicked[c, b : b + 1, where] = momenta[c, b : b + 1, where] + force
        return carry

    lax.fori_loop(0, tiles, body, 0)


def route_kernel(
    planes, neighbours, positions, momenta, noise, charges, route, cells, offsets,
    fields, sources, kicked, slot_out, field_send, field_recv, source_send, source_recv,
):
    grid_rank = lax.axis_index("grid")
    bead_rank = lax.axis_index("bead")
    rows = route[...]
    slot = slots_of(rows, BIN // planes)
    slot_out[...] = slot
    first = (rows * planes + cells[0:1]).astype(jnp.float32) + offsets[0:1]
    rest = cells[1:3].astype(jnp.float32) + offsets[1:3]
    own = jnp.concatenate([charges[...], first, rest], axis=0)
    halves = [part.astype(jnp.float32) for part in split3(own)]
    packed = jnp.concatenate(halves + [jnp.zeros_like(own)], axis=0).astype(jnp.bfloat16)
    got = lax.dot_general(packed, placement(slot), (NT, ((), ())), preferred_element_type=jnp.float32)
    fields[grid_rank] = (got[0:4] + got[4:8]) + got[8:12]
    sources[bead_rank, 0] = positions[...]
    sources[bead_rank, 1] = noise[...]

    greet(("grid", "bead"))
    move = shares("grid", lambda p: fields.at[grid_rank], lambda p: fields.at[p], field_send, field_recv)
    moved = shares("bead", lambda p: sources.at[bead_rank], lambda p: sources.at[p], source_send, source_recv)
    move[0]()
    moved[0]()

    def weight_of(t, m):
        total = 0.0
        for k in range(neighbours.shape[1]):
            total += jnp.where(neighbours[t, k] == m, 0.5 * time_step * pair_strength, 0.0)
        return total

    pair_forces(weight_of, positions, momenta, kicked)
    for step in (1, 2):
        move[step]()
        moved[step]()


def route_fields(positions, momenta, noise, charges, slab_route, cells, offsets, nbr_tiles):
    grid_count = lax.axis_size("grid")
    bead_count = lax.axis_size("bead")
    beads, atoms = positions.shape[1:]
    vmem = pl.BlockSpec(memory_space=pltpu.VMEM)
    dma = pltpu.SemaphoreType.DMA
    pairs = beads * atoms ** 2
    return pl.pallas_call(
        functools.partial(route_kernel, GX // grid_count),
        out_shape=[
            jax.ShapeDtypeStruct((grid_count, 4, GX // BIN * CAP), jnp.float32),
            jax.ShapeDtypeStruct((bead_count, 2, 3, beads, atoms), jnp.float32),
            jax.ShapeDtypeStruct((3, beads, atoms), jnp.float32),
            jax.ShapeDtypeStruct((1, atoms), jnp.int32),
        ],
        in_specs=[pl.BlockSpec(memory_space=pltpu.SMEM)] + [vmem] * 7,
        out_specs=[vmem] * 4,
        scratch_shapes=[dma((grid_count,)), dma((grid_count,)), dma((bead_count,)), dma((bead_count,))],
        compiler_params=pltpu.CompilerParams(
            collective_id=0, has_side_effects=True, vmem_limit_bytes=32 * 1024 * 1024
        ),
        cost_estimate=pl.CostEstimate(
            flops=20 * pairs, bytes_accessed=12 * positions.size, transcendentals=pairs
        ),
    )(
        nbr_tiles, positions, momenta, noise, charges.reshape(1, atoms),
        slab_route.reshape(1, atoms), cells, offsets,
    )


def step_tables(bead_total):
    mode = np.arange(bead_total)
    angle = (mode[:, None] * mode[None, :] % bead_total) * (2.0 * math.pi / bead_total)
    middle = bead_total // 2
    scaled = math.sqrt(2.0 / bead_total)
    column = mode[:, None]
    matrix = np.where(
        column == 0,
        1.0 / math.sqrt(bead_total),
        np.where(
            column < middle,
            scaled * np.cos(angle),
            np.where(
                column == middle, np.cos(angle) / math.sqrt(bead_total), scaled * np.sin(angle)
            ),
        ),
    )
    half = 0.5 * time_step
    frequency = 2.0 * polymer_frequency * np.sin(mode * (math.pi / bead_total))
    cosine = np.cos(frequency * half)
    drift = np.where(mode == 0, half, np.sin(frequency * half) / np.where(mode == 0, 1.0, frequency))
    pull = frequency * np.sin(frequency * half)
    friction = np.where(mode == 0, centroid_friction, 2.0 * frequency)
    damping = np.exp(-friction * time_step)
    kick = np.sqrt(1.0 - damping * damping)
    factors = [
        [cosine * cosine - drift * damping * pull, drift * cosine * (1.0 + damping), drift * kick],
        [-cosine * pull * (1.0 + damping), cosine * damping * cosine - pull * drift, cosine * kick],
    ]
    tables = np.stack(
        [
            np.stack(
                [
                    matrix.T @ (row[0][:, None] * matrix),
                    matrix.T @ (row[1][:, None] * matrix),
                    matrix.T * row[2][None, :],
                ]
            )
            for row in factors
        ]
    )
    return tables.astype(np.float32), (float(factors[0][1][0]), float(factors[1][1][0]))


def finish_kernel(
    centre, tables, partial, sources, kicked, slot, new_positions, new_momenta,
    landed, kicks, level, last, part_send, part_recv, kick_send, kick_recv, last_send, last_recv,
):
    grid_rank = lax.axis_index("grid")
    bead_rank = lax.axis_index("bead")
    bead_count = lax.axis_size("bead")
    domains = partial.shape[0]
    beads = kicked.shape[1]

    greet(("grid", "bead"))
    move = shares("grid", lambda p: partial.at[p], lambda p: landed.at[p], part_send, part_recv)
    moved = shares("bead", lambda p: kicked, lambda p: kicks.at[p], kick_send, kick_recv)
    summed = shares("bead", lambda p: level, lambda p: last.at[p], last_send, last_recv)
    move[0]()
    moved[0]()
    landed[grid_rank] = partial[grid_rank]
    kicks[bead_rank] = kicked[...]
    where = placement(slot[...])
    move[1]()
    total = landed[0]
    for d in range(1, domains):
        total = total + landed[d]
    level[...] = total
    last[bead_rank] = total
    summed[0]()

    moved[1]()
    own = tables[bead_rank]
    stepped = []
    for c in range(3):
        parts = [sources[k, 0, c] for k in range(bead_count)]
        parts += [kicks[k, c] for k in range(bead_count)]
        parts += [sources[k, 1, c] for k in range(bead_count)]
        stepped.append(
            jnp.dot(own, jnp.concatenate(parts, axis=0), precision=highest, preferred_element_type=jnp.float32)
        )
    summed[1]()
    total = last[0]
    for k in range(1, bead_count):
        total = total + last[k]
    halves = [part.astype(jnp.float32) for part in split3(total)]
    packed = jnp.concatenate(halves + [jnp.zeros((16 - 9, total.shape[1]), jnp.float32)], axis=0)
    got = jnp.dot(packed.astype(jnp.bfloat16), where, preferred_element_type=jnp.float32)
    force = (got[0:3] + got[3:6]) + got[6:9]
    for c in range(3):
        new_positions[c] = stepped[c][0:beads] + centre[0] * force[c : c + 1]
        new_momenta[c] = stepped[c][beads:] + centre[1] * force[c : c + 1]
    for each in (move, moved, summed):
        each[2]()


def finish(partial, sources, kicked, slot):
    grid_count = lax.axis_size("grid")
    bead_count = lax.axis_size("bead")
    beads, atoms = kicked.shape[1:]
    tables, centre = step_tables(beads * bead_count)
    shaped = tables.reshape(2, 3, bead_count, beads, -1).transpose(2, 0, 3, 1, 4)
    shaped = shaped.reshape(bead_count, 2 * beads, -1)
    centre = tuple(0.5 * time_step * value for value in centre)
    vmem = pl.BlockSpec(memory_space=pltpu.VMEM)
    dma = pltpu.SemaphoreType.DMA
    part = partial.shape[1:]
    return pl.pallas_call(
        functools.partial(finish_kernel, centre),
        out_shape=[jax.ShapeDtypeStruct(kicked.shape, jnp.float32)] * 2,
        in_specs=[vmem] * 5,
        out_specs=[vmem] * 2,
        scratch_shapes=[
            pltpu.VMEM((grid_count, *part), jnp.float32),
            pltpu.VMEM((bead_count, *kicked.shape), jnp.float32),
            pltpu.VMEM(part, jnp.float32),
            pltpu.VMEM((bead_count, *part), jnp.float32),
            dma((grid_count,)), dma((grid_count,)),
            dma((bead_count,)), dma((bead_count,)),
            dma((bead_count,)), dma((bead_count,)),
        ],
        compiler_params=pltpu.CompilerParams(
            collective_id=1, has_side_effects=True, vmem_limit_bytes=32 * 1024 * 1024
        ),
    )(jnp.asarray(shaped), partial, sources, kicked, slot)


def per_device(positions, momenta, noise, charges, slab_route, cells, offsets, nbr_tiles):
    fields, sources, kicked, slot = route_fields(
        positions, momenta, noise, charges, slab_route, cells, offsets, nbr_tiles
    )
    partial = mesh_forces(fields)
    return finish(partial, sources, kicked, slot)


def solution(mesh):
    in_specs = (
        P(None, "bead", "grid"),
        P(None, "bead", "grid"),
        P(None, "bead", "grid"),
        P("grid"),
        P("grid", None),
        P(None, "grid"),
        P(None, "grid"),
        P("grid", None),
    )
    out_specs = (P(None, "bead", "grid"), P(None, "bead", "grid"))

    def step(*args):
        return tuple(per_device(*args))

    return jax.shard_map(step, mesh=mesh, in_specs=in_specs, out_specs=out_specs, check_vma=False)
```

time: 118 us -> 64 us (0.54)
  Pallas kernels: 73.8 us -> 55.7 us
  blocking collectives: 13.6 us -> 0 us
  starting transfers between devices: 13.4 us -> 0 us
  waiting for transfers between devices: 5.74 us -> 0 us
  other arithmetic: 5.44 us -> 0 us
  local copies, waits for them, and re-layouts: 3.84 us -> 7.11 us
    pallas_call x2 -> x3, Pallas kernels: 73.8 us -> 55.7 us  [the longest x1 30.4 us: mesh_forces(): pl.pallas_call(functools.partial(mesh_kernel, axes), out_shape=jax.ShapeD...]
    all_to_all x2 -> x0, starting transfers between devices: 13.4 us -> none  [the longest x1 7.41 us: per_device(): lax.all_to_all(copies, 'grid', split_axis=1, concat_axis=1, tiled=True)]
    all_gather x1 -> x0, blocking collectives: 7.53 us -> none  [per_device(): lax.all_gather(jnp.stack([positions, kicked, noise]), 'bead', axis=2, til...]
    unnamed x12 -> x36, local copies, waits for them, and re-layouts: 0.02 us -> 7.11 us
    psum x1 -> x0, blocking collectives: 6.07 us -> none  [per_device(): mesh_force = half_step * lax.psum(jnp.sum(shares, axis=1), 'bead')]
    all_to_all x2 -> x0, waiting for transfers between devices: 5.74 us -> none  [the longest x1 5.74 us: per_device(): lax.all_to_all(partial.reshape(3, grid_count, charges.shape[0]), 'grid',...]
    dynamic_slice x6 -> x0, local copies, waits for them, and re-layouts: 3.03 us -> none  [rows_of(): return lax.dynamic_slice_in_dim(jnp.asarray(values), first, count, 0)]
    mul x4 -> x0, other arithmetic: 1.55 us -> none  [the longest x1 0.89 us: mesh_forces(): screen = screen * times]
  transfers between devices with their start and end apart: 2 -> 0, of which waited for: 1 -> 0; matrix products, arithmetic and copies ran while one was open for 6% -> 0% of each run, Pallas kernels for 7% -> 0%
where the time goes in v1:
time: 64 us; the launch traced here: 63.6 us
  Pallas kernels  55.7 us (87%)
  local copies, waits for them, and re-layouts  7.11 us (11%)
  between operations  0.79 us (1%)
    pallas_call x1, Pallas kernels, mesh_forces(): pl.pallas_call(functools.partial(mesh_kernel, axes), out_shape=jax.ShapeD...  30.4 us
    pallas_call x1, Pallas kernels, route_fields(): pl.pallas_call(functools.partial(route_kernel, GX // grid_count), out_sha...  14.8 us
    pallas_call x1, Pallas kernels, finish(): pl.pallas_call(functools.partial(finish_kernel, centre), out_shape=[jax.S...  10.4 us
    unnamed x36, local copies, waits for them, and re-layouts  7.11 us

profile of v1, /device:TPU:0, one launch (start us, length us, event | category | flops | bytes accessed | tf_op | source)
XLA Modules:
  0.0 63.6 jit_solution(5969762212777627109)
XLA Ops:
  0.6 0.0 copy-start.14
  0.6 0.7 %copy-done.14 = s32[4,4]{1,0:T(4,128)S(1)} copy-done((s32[4,4]{1,0:T(4,128)S(1)}, s32[4,4]{1,0:T(4,128)}, u32[]{:S(2)}) %copy-start.14) | copy-done | bytes 88
  1.3 0.0 copy-start.9
  1.3 0.8 %copy-done.9 = f32[3,8,512]{2,1,0:T(8,128)S(1)} copy-done((f32[3,8,512]{2,1,0:T(8,128)S(1)}, f32[3,8,512]{2,1,0:T(8,128)}, u32[]{:S(2)}) %copy-start.9) | copy-done | bytes 49176
  2.1 0.0 copy-start.10
  2.1 0.8 %copy-done.10 = f32[3,8,512]{2,1,0:T(8,128)S(1)} copy-done((f32[3,8,512]{2,1,0:T(8,128)S(1)}, f32[3,8,512]{2,1,0:T(8,128)}, u32[]{:S(2)}) %copy-start.10) | copy-done | bytes 49176
  2.9 0.0 copy-start.11
  2.9 0.8 %copy-done.11 = f32[3,8,512]{2,1,0:T(8,128)S(1)} copy-done((f32[3,8,512]{2,1,0:T(8,128)S(1)}, f32[3,8,512]{2,1,0:T(8,128)}, u32[]{:S(2)}) %copy-start.11) | copy-done | bytes 49176
  3.7 0.0 copy-start.12
  3.7 0.7 %copy-done.12 = s32[3,512]{1,0:T(4,128)S(1)} copy-done((s32[3,512]{1,0:T(4,128)S(1)}, s32[3,512]{1,0:T(4,128)}, u32[]{:S(2)}) %copy-start.12) | copy-done | bytes 6168
  4.4 0.7 %copy-done.13 = f32[3,512]{1,0:T(4,128)S(1)} copy-done((f32[3,512]{1,0:T(4,128)S(1)}, f32[3,512]{1,0:T(4,128)}, u32[]{:S(2)}) %copy-start.13) | copy-done | bytes 6168
  5.1 0.7 %copy-done.15 = f32[512]{0:T(512)S(1)} copy-done((f32[512]{0:T(512)S(1)}, f32[512]{0:T(512)}, u32[]{:S(2)}) %copy-start.15) | copy-done | bytes 2072
  5.8 0.7 %copy-done.16 = s32[512,1]{0,1:T(1,128)S(1)} copy-done((s32[512,1]{0,1:T(1,128)S(1)}, s32[512,1]{0,1:T(1,128)}, u32[]{:S(2)}) %copy-start.16) | copy-done | bytes 2072
  6.5 0.0 copy-start.4
  6.5 0.0 copy-start.5
  6.5 0.0 copy-start.6
  6.5 0.0 copy-start.7
  6.5 14.8 %shard_map.176 = (f32[8,4,1024]{2,1,0:T(4,128)S(1)}, f32[4,2,3,8,512]{4,3,2,1,0:T(8,128)S(1)}, f32[3,8,512]{2,1,0:T(8,128)S(1)}, s32[1,512]{1,0:T(1,128)S(1)}) custom-call(s32[4,4]{1,0:T(4,128)S(1)} %copy-done.14, f32[3,8,512]{2,1,0:T(8,128)S(1)} %copy-done.9, f32[3,8,512]{2,1,0:T(8,128)S(1)} %copy-done.10, f32[3,8,512]{2,1,0:T(8,128)S(1)} %copy-done.11, ...), custom_call_target="tpu_custom_call" | custom-call | flops 41943040 | bytes 147456 | tf_op jit(solution)/shard_map/pallas_call | solution.py:420
  21.4 0.0 copy-done
  21.4 0.0 copy-done.1
  21.4 0.0 copy-done.2
  21.4 0.0 copy-done.3
  21.4 0.0 copy-done.4
  21.4 0.0 copy-done.5
  21.4 0.0 copy-done.6
  21.4 0.0 copy-done.7
  21.4 0.0 copy-start.8
  21.5 30.4 %shard_map.177.partial = f32[8,3,1024]{2,1,0:T(4,128)S(1)} custom-call(f32[8,4,1024]{2,1,0:T(4,128)S(1)} %get-tuple-element.6.fields, bf16[256,256]{1,0:T(8,128)(2,1)S(1)} %copy-done.7, bf16[256,256]{1,0:T(8,128)(2,1)S(1)} %copy-done.6, bf16[256,256]{1,0:T(8,128)(2,1)S(1)} %copy-done.5, bf16[256,256]{1,0:T(8,128)(2,1)S(1)} %copy-done.4, ...), custom_call_target="tpu_custom_call" | custom-call | tf_op jit(solution)/shard_map/pallas_call | solution.py:242
  51.9 0.0 copy-done.8
  51.9 10.4 %shard_map.178 = (f32[3,8,512]{2,1,0:T(8,128)S(1)}, f32[3,8,512]{2,1,0:T(8,128)S(1)}) custom-call(f32[4,16,96]{2,1,0:T(8,128)S(1)} %copy-done.8, f32[8,3,1024]{2,1,0:T(4,128)S(1)} %shard_map.177.partial, f32[4,2,3,8,512]{4,3,2,1,0:T(8,128)S(1)} %get-tuple-element.7.sources, f32[3,8,512]{2,1,0:T(8,128)S(1)} %get-tuple-element.8.kicked, ...), custom_call_target="tpu_custom_call" | custom-call | tf_op jit(solution)/shard_map/pallas_call | solution.py:550
  62.3 0.6 copy.21
  62.9 0.6 copy.22
  (7 shorter events, 0.0 us)
Async XLA Ops:
  0.6 0.7 %copy-start.14 = (s32[4,4]{1,0:T(4,128)S(1)}, s32[4,4]{1,0:T(4,128)}, u32[]{:S(2)}) copy-start(s32[4,4]{1,0:T(4,128)} %neighbours.1) | copy-start | bytes 196
  1.3 0.8 %copy-start.9 = (f32[3,8,512]{2,1,0:T(8,128)S(1)}, f32[3,8,512]{2,1,0:T(8,128)}, u32[]{:S(2)}) copy-start(f32[3,8,512]{2,1,0:T(8,128)} %positions.1) | copy-start | bytes 147460
  2.1 0.8 %copy-start.10 = (f32[3,8,512]{2,1,0:T(8,128)S(1)}, f32[3,8,512]{2,1,0:T(8,128)}, u32[]{:S(2)}) copy-start(f32[3,8,512]{2,1,0:T(8,128)} %momenta.1) | copy-start | bytes 147460
  2.9 0.8 %copy-start.11 = (f32[3,8,512]{2,1,0:T(8,128)S(1)}, f32[3,8,512]{2,1,0:T(8,128)}, u32[]{:S(2)}) copy-start(f32[3,8,512]{2,1,0:T(8,128)} %noise.1) | copy-start | bytes 147460
  3.7 0.7 %copy-start.12 = (s32[3,512]{1,0:T(4,128)S(1)}, s32[3,512]{1,0:T(4,128)}, u32[]{:S(2)}) copy-start(s32[3,512]{1,0:T(4,128)} %cells.1) | copy-start | bytes 18436
  4.4 0.7 %copy-start.13 = (f32[3,512]{1,0:T(4,128)S(1)}, f32[3,512]{1,0:T(4,128)}, u32[]{:S(2)}) copy-start(f32[3,512]{1,0:T(4,128)} %offsets.1) | copy-start | bytes 18436
  5.1 0.7 %copy-start.15 = (f32[512]{0:T(512)S(1)}, f32[512]{0:T(512)}, u32[]{:S(2)}) copy-start(f32[512]{0:T(512)} %param.20) | copy-start | bytes 6148
  5.8 0.7 %copy-start.16 = (s32[512,1]{0,1:T(1,128)S(1)}, s32[512,1]{0,1:T(1,128)}, u32[]{:S(2)}) copy-start(s32[512,1]{0,1:T(1,128)} %param.21) | copy-start | bytes 6148
  6.5 14.9 %copy-start = (bf16[256,256]{1,0:T(8,128)(2,1)S(1)}, bf16[256,256]{1,0:T(8,128)(2,1)}, u32[]{:S(2)}) copy-start(bf16[256,256]{1,0:T(8,128)(2,1)} %constant.25.clone.rtl) | copy-start | bytes 393220
  6.5 14.9 %copy-start.1 = (bf16[256,256]{1,0:T(8,128)(2,1)S(1)}, bf16[256,256]{1,0:T(8,128)(2,1)}, u32[]{:S(2)}) copy-start(bf16[256,256]{1,0:T(8,128)(2,1)} %constant.24.clone.rth) | copy-start | bytes 393220
  6.5 14.9 %copy-start.2 = (bf16[256,256]{1,0:T(8,128)(2,1)S(1)}, bf16[256,256]{1,0:T(8,128)(2,1)}, u32[]{:S(2)}) copy-start(bf16[256,256]{1,0:T(8,128)(2,1)} %constant.23.clone.rl) | copy-start | bytes 393220
  6.5 14.9 %copy-start.3 = (bf16[256,256]{1,0:T(8,128)(2,1)S(1)}, bf16[256,256]{1,0:T(8,128)(2,1)}, u32[]{:S(2)}) copy-start(bf16[256,256]{1,0:T(8,128)(2,1)} %constant.22.clone.rh) | copy-start | bytes 393220
  6.5 14.9 %copy-start.4 = (bf16[256,256]{1,0:T(8,128)(2,1)S(1)}, bf16[256,256]{1,0:T(8,128)(2,1)}, u32[]{:S(2)}) copy-start(bf16[256,256]{1,0:T(8,128)(2,1)} %constant.21.clone.fxtl) | copy-start | bytes 393220
  6.5 14.9 %copy-start.5 = (bf16[256,256]{1,0:T(8,128)(2,1)S(1)}, bf16[256,256]{1,0:T(8,128)(2,1)}, u32[]{:S(2)}) copy-start(bf16[256,256]{1,0:T(8,128)(2,1)} %constant.20.clone.fxth) | copy-start | bytes 393220
  6.5 14.9 %copy-start.6 = (bf16[256,256]{1,0:T(8,128)(2,1)S(1)}, bf16[256,256]{1,0:T(8,128)(2,1)}, u32[]{:S(2)}) copy-start(bf16[256,256]{1,0:T(8,128)(2,1)} %constant.19.clone.fxl) | copy-start | bytes 393220
  6.5 14.9 %copy-start.7 = (bf16[256,256]{1,0:T(8,128)(2,1)S(1)}, bf16[256,256]{1,0:T(8,128)(2,1)}, u32[]{:S(2)}) copy-start(bf16[256,256]{1,0:T(8,128)(2,1)} %constant.18.clone.fxh) | copy-start | bytes 393220
  21.4 30.4 %copy-start.8 = (f32[4,16,96]{2,1,0:T(8,128)S(1)}, f32[4,16,96]{2,1,0:T(8,128)}, u32[]{:S(2)}) copy-start(f32[4,16,96]{2,1,0:T(8,128)} %constant.26.clone.tables) | copy-start | bytes 73732

commit v2 on v1

--- a/solution.py
+++ b/solution.py
@@ -127,13 +127,13 @@
         phase = phase + wave
     return (value, slope) if with_slope else (value,)
 
-def mesh_kernel(axes, fields, fxh, fxl, fxth, fxtl, rh, rl, rth, rtl, out, total, filt, wave2):
+def mesh_phases(fields, tables, out, total, filt, wave2, ready):
     domains = fields.shape[0]
-    grid_name, bead_name = axes
-    bead_count = lax.axis_size(bead_name)
-    device = lax.axis_index(grid_name) * bead_count + lax.axis_index(bead_name)
+    bead_count = lax.axis_size("bead")
+    device = lax.axis_index("grid") * bead_count + lax.axis_index("bead")
+    fx, fxt, rt, back = [tables.at[i] for i in range(4)]
     groups = GY // WAVES
-    parts = lax.axis_size(grid_name) * bead_count // groups
+    parts = lax.axis_size("grid") * bead_count // groups
     group = lax.rem(device, groups)
     part = lax.div(device, groups)
     bins = GX // BIN
@@ -179,6 +179,8 @@
         return carry
     lax.fori_loop(0, bins * chunks, spread, 0)
 
+    ready()
+
     def transform(r, carry):
         wave, _ = wave_of_row(group, r)
         wave = jnp.full((1, GZ), wave, jnp.int32)
@@ -186,12 +188,12 @@
         count = jnp.where((wave & (GY // 2 - 1)) == 0, 1.0, 2.0)
         scale = count * jnp.exp(wave_square * (-1.0 / (2.0 * screen_width * screen_width))) * (coulomb_scale / (GX * GY * GZ))
         total[r, 0:8, :] += total[r, GX:GX + 8, :]
-        t = dot3((fxh[...], fxl[...]), split(total[r, 0:GX, :]), NN)
-        t = dot3(split(t), (rth[...], rtl[...]), NN)
+        t = dot3((fx[0], fx[1]), split(total[r, 0:GX, :]), NN)
+        t = dot3(split(t), (rt[0], rt[1]), NN)
         m2 = wave2[...] + wave_square
         t = t * jnp.where(m2 == 0.0, 0.0, filt[...] * scale / jnp.where(m2 == 0.0, 1.0, m2))
-        t = dot3(split(t), (rh[...], rl[...]), NN)
-        t = dot3((fxth[...], fxtl[...]), split(t), NN)
+        t = dot3(split(t), (back[0], back[1]), NN)
+        t = dot3((fxt[0], fxt[1]), split(t), NN)
         total[r, 0:GX, :] = t
         total[r, GX:GX + 8, :] = t[0:8]
         return carry
@@ -231,26 +233,11 @@
     wave = jnp.where(odd, GY // 2, group * half + (row & (half - 1)))
     return wave, odd
 
-def mesh_forces(fields, axes=("grid", "bead")):
-    domains = fields.shape[0]
+
+def wave_tables():
     table = real_waves(GX)
     shifted = np.roll(table, 1, axis=1)
-    tables = []
-    for t in (shifted, shifted.T, table, table.T):
-        tables += [jnp.asarray(v) for v in split_table(t)]
-    vmem = pl.BlockSpec(memory_space=pltpu.VMEM)
-    return pl.pallas_call(
-        functools.partial(mesh_kernel, axes),
-        out_shape=jax.ShapeDtypeStruct((domains, 3, GX // BIN * CAP), jnp.float32),
-        in_specs=[vmem] * 9,
-        out_specs=vmem,
-        scratch_shapes=[
-            pltpu.VMEM((WAVES, GX + 8, GZ), jnp.float32),
-            pltpu.VMEM((GX, GZ), jnp.float32),
-            pltpu.VMEM((GX, GZ), jnp.float32),
-        ],
-        compiler_params=pltpu.CompilerParams(vmem_limit_bytes=48 * 1024 * 1024),
-    )(fields, *tables)
+    return jnp.stack([jnp.stack(split_table(t)) for t in (shifted, shifted.T, table.T, table)])
 
 
 TILE = 128
@@ -371,73 +358,6 @@
         return carry
 
     lax.fori_loop(0, tiles, body, 0)
-
-
-def route_kernel(
-    planes, neighbours, positions, momenta, noise, charges, route, cells, offsets,
-    fields, sources, kicked, slot_out, field_send, field_recv, source_send, source_recv,
-):
-    grid_rank = lax.axis_index("grid")
-    bead_rank = lax.axis_index("bead")
-    rows = route[...]
-    slot = slots_of(rows, BIN // planes)
-    slot_out[...] = slot
-    first = (rows * planes + cells[0:1]).astype(jnp.float32) + offsets[0:1]
-    rest = cells[1:3].astype(jnp.float32) + offsets[1:3]
-    own = jnp.concatenate([charges[...], first, rest], axis=0)
-    halves = [part.astype(jnp.float32) for part in split3(own)]
-    packed = jnp.concatenate(halves + [jnp.zeros_like(own)], axis=0).astype(jnp.bfloat16)
-    got = lax.dot_general(packed, placement(slot), (NT, ((), ())), preferred_element_type=jnp.float32)
-    fields[grid_rank] = (got[0:4] + got[4:8]) + got[8:12]
-    sources[bead_rank, 0] = positions[...]
-    sources[bead_rank, 1] = noise[...]
-
-    greet(("grid", "bead"))
-    move = shares("grid", lambda p: fields.at[grid_rank], lambda p: fields.at[p], field_send, field_recv)
-    moved = shares("bead", lambda p: sources.at[bead_rank], lambda p: sources.at[p], source_send, source_recv)
-    move[0]()
-    moved[0]()
-
-    def weight_of(t, m):
-        total = 0.0
-        for k in range(neighbours.shape[1]):
-            total += jnp.where(neighbours[t, k] == m, 0.5 * time_step * pair_strength, 0.0)
-        return total
-
-    pair_forces(weight_of, positions, momenta, kicked)
-    for step in (1, 2):
-        move[step]()
-        moved[step]()
-
-
-def route_fields(positions, momenta, noise, charges, slab_route, cells, offsets, nbr_tiles):
-    grid_count = lax.axis_size("grid")
-    bead_count = lax.axis_size("bead")
-    beads, atoms = positions.shape[1:]
-    vmem = pl.BlockSpec(memory_space=pltpu.VMEM)
-    dma = pltpu.SemaphoreType.DMA
-    pairs = beads * atoms ** 2
-    return pl.pallas_call(
-        functools.partial(route_kernel, GX // grid_count),
-        out_shape=[
-            jax.ShapeDtypeStruct((grid_count, 4, GX // BIN * CAP), jnp.float32),
-            jax.ShapeDtypeStruct((bead_count, 2, 3, beads, atoms), jnp.float32),
-            jax.ShapeDtypeStruct((3, beads, atoms), jnp.float32),
-            jax.ShapeDtypeStruct((1, atoms), jnp.int32),
-        ],
-        in_specs=[pl.BlockSpec(memory_space=pltpu.SMEM)] + [vmem] * 7,
-        out_specs=[vmem] * 4,
-        scratch_shapes=[dma((grid_count,)), dma((grid_count,)), dma((bead_count,)), dma((bead_count,))],
-        compiler_params=pltpu.CompilerParams(
-            collective_id=0, has_side_effects=True, vmem_limit_bytes=32 * 1024 * 1024
-        ),
-        cost_estimate=pl.CostEstimate(
-            flops=20 * pairs, bytes_accessed=12 * positions.size, transcendentals=pairs
-        ),
-    )(
-        nbr_tiles, positions, momenta, noise, charges.reshape(1, atoms),
-        slab_route.reshape(1, atoms), cells, offsets,
-    )
 
 
 def step_tables(bead_total):
@@ -484,95 +404,152 @@
     return tables.astype(np.float32), (float(factors[0][1][0]), float(factors[1][1][0]))
 
 
-def finish_kernel(
-    centre, tables, partial, sources, kicked, slot, new_positions, new_momenta,
-    landed, kicks, level, last, part_send, part_recv, kick_send, kick_recv, last_send, last_recv,
+def step_kernel(
+    planes, centre, neighbours, positions, momenta, noise, charges, route, cells, offsets, mixing, waves,
+    new_positions, new_momenta,
+    own_momenta, own_charges, own_route, own_cells, own_offsets, own_mixing, own_waves,
+    fields, sources, kicks, partial, landed, level, last, total, filt, wave2,
+    local_sem, field_send, field_recv, place_send, place_recv, noise_send, noise_recv,
+    kick_send, kick_recv, part_send, part_recv, last_send, last_recv,
 ):
     grid_rank = lax.axis_index("grid")
     bead_rank = lax.axis_index("bead")
     bead_count = lax.axis_size("bead")
     domains = partial.shape[0]
-    beads = kicked.shape[1]
+    beads = kicks.shape[2]
+
+    pairs = [
+        (route, own_route), (charges, own_charges), (cells, own_cells), (offsets, own_offsets),
+        (positions, sources.at[bead_rank, 0]), (momenta, own_momenta),
+        (noise, sources.at[bead_rank, 1]), (mixing, own_mixing), (waves, own_waves),
+    ]
+    loads = [pltpu.make_async_copy(a, b, local_sem.at[i]) for i, (a, b) in enumerate(pairs)]
+    for load in loads:
+        load.start()
+    for load in loads[0:4]:
+        load.wait()
+
+    rows = own_route[...]
+    slot = slots_of(rows, BIN // planes)
+    first = (rows * planes + own_cells[0:1]).astype(jnp.float32) + own_offsets[0:1]
+    rest = own_cells[1:3].astype(jnp.float32) + own_offsets[1:3]
+    own = jnp.concatenate([own_charges[...], first, rest], axis=0)
+    halves = [part.astype(jnp.float32) for part in split3(own)]
+    packed = jnp.concatenate(halves + [jnp.zeros_like(own)], axis=0).astype(jnp.bfloat16)
+    got = lax.dot_general(packed, placement(slot), (NT, ((), ())), preferred_element_type=jnp.float32)
+    fields[grid_rank] = (got[0:4] + got[4:8]) + got[8:12]
 
     greet(("grid", "bead"))
-    move = shares("grid", lambda p: partial.at[p], lambda p: landed.at[p], part_send, part_recv)
-    moved = shares("bead", lambda p: kicked, lambda p: kicks.at[p], kick_send, kick_recv)
+    field = shares("grid", lambda p: fields.at[grid_rank], lambda p: fields.at[p], field_send, field_recv)
+    place = shares("bead", lambda p: positions, lambda p: sources.at[p, 0], place_send, place_recv)
+    draw = shares("bead", lambda p: noise, lambda p: sources.at[p, 1], noise_send, noise_recv)
+    kick = shares("bead", lambda p: kicks.at[bead_rank], lambda p: kicks.at[p], kick_send, kick_recv)
+    part = shares("grid", lambda p: partial.at[p], lambda p: landed.at[p], part_send, part_recv)
     summed = shares("bead", lambda p: level, lambda p: last.at[p], last_send, last_recv)
-    move[0]()
-    moved[0]()
+    for each in (field, place, draw):
+        each[0]()
+
+    def weight_of(t, m):
+        total = 0.0
+        for k in range(neighbours.shape[1]):
+            total += jnp.where(neighbours[t, k] == m, 0.5 * time_step * pair_strength, 0.0)
+        return total
+
+    loads[4].wait()
+    loads[5].wait()
+    pair_forces(weight_of, sources.at[bead_rank, 0], own_momenta, kicks.at[bead_rank])
+    kick[0]()
+    field[1]()
+
+    mesh_phases(fields, own_waves, partial, total, filt, wave2, loads[8].wait)
+    part[0]()
+
     landed[grid_rank] = partial[grid_rank]
-    kicks[bead_rank] = kicked[...]
-    where = placement(slot[...])
-    move[1]()
-    total = landed[0]
-    for d in range(1, domains):
-        total = total + landed[d]
-    level[...] = total
-    last[bead_rank] = total
-    summed[0]()
-
-    moved[1]()
-    own = tables[bead_rank]
-    stepped = []
-    for c in range(3):
+    where = placement(slot)
+    for each in (place, draw, kick):
+        each[1]()
+    loads[6].wait()
+    loads[7].wait()
+    mix = own_mixing[bead_rank]
+
+    def stepped(c):
         parts = [sources[k, 0, c] for k in range(bead_count)]
         parts += [kicks[k, c] for k in range(bead_count)]
         parts += [sources[k, 1, c] for k in range(bead_count)]
-        stepped.append(
-            jnp.dot(own, jnp.concatenate(parts, axis=0), precision=highest, preferred_element_type=jnp.float32)
-        )
+        got = jnp.dot(mix, jnp.concatenate(parts, axis=0), precision=highest, preferred_element_type=jnp.float32)
+        new_positions[c] = got[0:beads]
+        new_momenta[c] = got[beads:]
+
+    stepped(0)
+    part[1]()
+    forces = landed[0]
+    for d in range(1, domains):
+        forces = forces + landed[d]
+    level[...] = forces
+    last[bead_rank] = forces
+    summed[0]()
+    stepped(1)
+    stepped(2)
     summed[1]()
-    total = last[0]
+    forces = last[0]
     for k in range(1, bead_count):
-        total = total + last[k]
-    halves = [part.astype(jnp.float32) for part in split3(total)]
-    packed = jnp.concatenate(halves + [jnp.zeros((16 - 9, total.shape[1]), jnp.float32)], axis=0)
+        forces = forces + last[k]
+    halves = [part.astype(jnp.float32) for part in split3(forces)]
+    packed = jnp.concatenate(halves + [jnp.zeros((16 - 9, forces.shape[1]), jnp.float32)], axis=0)
     got = jnp.dot(packed.astype(jnp.bfloat16), where, preferred_element_type=jnp.float32)
     force = (got[0:3] + got[3:6]) + got[6:9]
     for c in range(3):
-        new_positions[c] = stepped[c][0:beads] + centre[0] * force[c : c + 1]
-        new_momenta[c] = stepped[c][beads:] + centre[1] * force[c : c + 1]
-    for each in (move, moved, summed):
+        new_positions[c] += centre[0] * force[c : c + 1]
+        new_momenta[c] += centre[1] * force[c : c + 1]
+    for each in (field, place, draw, kick, part, summed):
         each[2]()
 
 
-def finish(partial, sources, kicked, slot):
+def per_device(positions, momenta, noise, charges, slab_route, cells, offsets, nbr_tiles):
     grid_count = lax.axis_size("grid")
     bead_count = lax.axis_size("bead")
-    beads, atoms = kicked.shape[1:]
+    beads, atoms = positions.shape[1:]
+    slots = GX // BIN * CAP
     tables, centre = step_tables(beads * bead_count)
     shaped = tables.reshape(2, 3, bead_count, beads, -1).transpose(2, 0, 3, 1, 4)
-    shaped = shaped.reshape(bead_count, 2 * beads, -1)
+    shaped = jnp.asarray(shaped.reshape(bead_count, 2 * beads, -1))
     centre = tuple(0.5 * time_step * value for value in centre)
+    waves = wave_tables()
     vmem = pl.BlockSpec(memory_space=pltpu.VMEM)
+    anywhere = pl.BlockSpec(memory_space=pl.ANY)
     dma = pltpu.SemaphoreType.DMA
-    part = partial.shape[1:]
+    whole = lambda array: pltpu.VMEM(array.shape, array.dtype)
+    f32 = lambda *shape: pltpu.VMEM(shape, jnp.float32)
+    charges = charges.reshape(1, atoms)
+    slab_route = slab_route.reshape(1, atoms)
     return pl.pallas_call(
-        functools.partial(finish_kernel, centre),
-        out_shape=[jax.ShapeDtypeStruct(kicked.shape, jnp.float32)] * 2,
-        in_specs=[vmem] * 5,
+        functools.partial(step_kernel, GX // grid_count, centre),
+        out_shape=[jax.ShapeDtypeStruct(positions.shape, jnp.float32)] * 2,
+        in_specs=[pl.BlockSpec(memory_space=pltpu.SMEM)] + [anywhere] * 9,
         out_specs=[vmem] * 2,
         scratch_shapes=[
-            pltpu.VMEM((grid_count, *part), jnp.float32),
-            pltpu.VMEM((bead_count, *kicked.shape), jnp.float32),
-            pltpu.VMEM(part, jnp.float32),
-            pltpu.VMEM((bead_count, *part), jnp.float32),
+            whole(momenta), whole(charges), whole(slab_route), whole(cells), whole(offsets),
+            whole(shaped), whole(waves),
+            f32(grid_count, 4, slots),
+            f32(bead_count, 2, *positions.shape),
+            f32(bead_count, *positions.shape),
+            f32(grid_count, 3, slots),
+            f32(grid_count, 3, slots),
+            f32(3, slots),
+            f32(bead_count, 3, slots),
+            f32(WAVES, GX + 8, GZ),
+            f32(GX, GZ),
+            f32(GX, GZ),
+            dma((9,)),
             dma((grid_count,)), dma((grid_count,)),
-            dma((bead_count,)), dma((bead_count,)),
-            dma((bead_count,)), dma((bead_count,)),
+            *[dma((bead_count,)) for _ in range(6)],
+            dma((grid_count,)), dma((grid_count,)),
+            *[dma((bead_count,)) for _ in range(2)],
         ],
         compiler_params=pltpu.CompilerParams(
-            collective_id=1, has_side_effects=True, vmem_limit_bytes=32 * 1024 * 1024
+            collective_id=0, has_side_effects=True, vmem_limit_bytes=60 * 1024 * 1024
         ),
-    )(jnp.asarray(shaped), partial, sources, kicked, slot)
-
-
-def per_device(positions, momenta, noise, charges, slab_route, cells, offsets, nbr_tiles):
-    fields, sources, kicked, slot = route_fields(
-        positions, momenta, noise, charges, slab_route, cells, offsets, nbr_tiles
-    )
-    partial = mesh_forces(fields)
-    return finish(partial, sources, kicked, slot)
+    )(nbr_tiles, positions, momenta, noise, charges, slab_route, cells, offsets, shaped, waves)
 
 
 def solution(mesh):

time: 64 us -> 56.9 us (0.89)
  local copies, waits for them, and re-layouts: 7.11 us -> 2.06 us
  Pallas kernels: 55.7 us -> 53.9 us
    unnamed x36 -> x4, local copies, waits for them, and re-layouts: 7.11 us -> 2.06 us
    pallas_call x3 -> x1, Pallas kernels: 55.7 us -> 53.9 us  [per_device(): pl.pallas_call(functools.partial(step_kernel, GX // grid_count, centre),...]
where the time goes in v2:
time: 56.9 us; the launch traced here: 56.7 us
  Pallas kernels  53.9 us (95%)
  local copies, waits for them, and re-layouts  2.06 us (4%)
  between operations  0.65 us (1%)
    pallas_call x1, Pallas kernels, per_device(): pl.pallas_call(functools.partial(step_kernel, GX // grid_count, centre),...  53.9 us
    unnamed x4, local copies, waits for them, and re-layouts  2.06 us

profile of v2, /device:TPU:0, one launch (start us, length us, event | category | flops | bytes accessed | tf_op | source)
XLA Modules:
  0.0 56.7 jit_solution(17949119095231315890)
XLA Ops:
  0.6 53.9 %shard_map.176 = (f32[3,8,512]{2,1,0:T(8,128)}, f32[3,8,512]{2,1,0:T(8,128)}) custom-call(s32[4,4]{1,0:T(4,128)} %neighbours.1, f32[3,8,512]{2,1,0:T(8,128)} %positions.1, f32[3,8,512]{2,1,0:T(8,128)} %momenta.1, f32[3,8,512]{2,1,0:T(8,128)} %noise.1, f32[1,512]{1,0:T(1,128)} %bitcast.2, s32[1,512]{1,0:T(1,128)} %bitcast.3, s32[3,512]{1,0:T(4,128)} %cells.1, ...), custom_call_target="tpu_custom_call" | custom-call | tf_op jit(solution)/shard_map/pallas_call | solution.py:525
  54.6 0.0 copy-start
  54.6 1.4 %copy.21 = f32[3,8,512]{2,1,0:T(8,128)} copy(f32[3,8,512]{2,1,0:T(8,128)} %get-tuple-element.4) | data formatting | bytes 98304
  56.0 0.0 copy-done
  56.0 0.6 %copy.22 = f32[3,8,512]{2,1,0:T(8,128)} copy(f32[3,8,512]{2,1,0:T(8,128)S(1)} %copy-done) | data formatting | bytes 98304
Async XLA Ops:
  54.6 1.4 %copy-start = (f32[3,8,512]{2,1,0:T(8,128)S(1)}, f32[3,8,512]{2,1,0:T(8,128)}, u32[]{:S(2)}) copy-start(f32[3,8,512]{2,1,0:T(8,128)} %get-tuple-element.5) | copy-start | bytes 147460

commit v3 on v2

--- a/solution.py
+++ b/solution.py
@@ -12,7 +12,7 @@
 GX = GY = GZ = 256
 WAVES = 8
 BIN = 32
-WINDOW = 40
+WINDOW = 36
 CAP = 128
 coulomb_scale = 100000.0
 screen_width = 200.0
@@ -60,40 +60,44 @@
         return lax.dot_general(a, b, (dims, ((), ())), preferred_element_type=jnp.float32)
     return one(left[0], right[0]) + (one(left[0], right[1]) + one(left[1], right[0]))
 
-def stencil(position, length, with_slope):
-    lowest = jnp.floor(position)
-    values, slopes = spline(position - lowest)
-    cell = lax.broadcasted_iota(jnp.int32, (length, position.shape[1]), 0)
-    step = (cell - (lowest.astype(jnp.int32) - 1)) & (length - 1)
-    step = step.astype(jnp.int16)
-    hits = [step == jnp.asarray(offset, step.dtype) for offset in range(4)]
-
-    def dense(members):
-        out = jnp.zeros(step.shape, jnp.bfloat16)
+def tracks(fields):
+    lowest = jnp.floor(fields)
+    values, slopes = spline(fields - lowest)
+    return [lowest, *values, *slopes]
+
+
+def stencil(cells, members, length):
+    row = lax.broadcasted_iota(jnp.int32, (length, cells.shape[1]), 0).astype(jnp.int16)
+    hits = []
+    for offset in range(4):
+        cell = ((cells + (offset - 1)) & (length - 1)).astype(jnp.int16)
+        hits.append(row == cell)
+
+    def dense(rows):
+        out = jnp.zeros(row.shape, jnp.bfloat16)
         for offset in range(4):
-            out = jnp.where(hits[offset], members[offset], out)
+            out = jnp.where(hits[offset], rows[offset], out)
         return out
 
-    def both(members):
-        halves = [split(member) for member in members]
-        return dense([half[0] for half in halves]), dense([half[1] for half in halves])
-
-    return (both(values), both(slopes)) if with_slope else (both(values),)
-
-def window(position, base, with_slope):
-    lowest = jnp.floor(position)
-    values, slopes = spline(position - lowest)
-    cell = lax.broadcasted_iota(jnp.int32, (WINDOW, position.shape[1]), 0)
-    step = cell - (lowest.astype(jnp.int32) - base)
-    hits = [step == offset for offset in range(4)]
-
-    def dense(members):
-        out = jnp.zeros(step.shape, jnp.float32)
+    found = []
+    for rows in members:
+        halves = [split(each) for each in rows]
+        found.append((dense([half[0] for half in halves]), dense([half[1] for half in halves])))
+    return found
+
+
+def window(cells, members):
+    row = lax.broadcasted_iota(jnp.int32, (WINDOW, cells.shape[1]), 0)
+    hits = [row == cells + offset for offset in range(4)]
+
+    def dense(rows):
+        out = jnp.zeros(row.shape, jnp.float32)
         for offset in range(4):
-            out = jnp.where(hits[offset], members[offset], out)
+            out = jnp.where(hits[offset], rows[offset], out)
         return out
 
-    return (dense(values), dense(slopes)) if with_slope else (dense(values),)
+    return [dense(rows) for rows in members]
+
 
 def wave_of(group, shape):
     row = lax.broadcasted_iota(jnp.int32, shape, 0)
@@ -113,21 +117,18 @@
         total = total * square + sign / power
     return -(angle * total)
 
-def lines(position, group, with_slope):
-    lowest = jnp.floor(position)
-    values, slopes = spline(position - lowest)
-    wave, turn = wave_of(group, (WAVES, position.shape[1]))
-    phase = wave * (lowest.astype(jnp.int32) - 1) + turn
-    value = slope = 0.0
+def lines(cells, members, group):
+    wave, turn = wave_of(group, (WAVES, cells.shape[1]))
+    phase = wave * (cells - 1) + turn
+    found = [0.0 for _ in members]
     for offset in range(4):
         cosine = turned(phase)
-        value = value + values[offset] * cosine
-        if with_slope:
-            slope = slope + slopes[offset] * cosine
+        found = [total + rows[offset] * cosine for total, rows in zip(found, members)]
         phase = phase + wave
-    return (value, slope) if with_slope else (value,)
-
-def mesh_phases(fields, tables, out, total, filt, wave2, ready):
+    return found
+
+
+def mesh_phases(fields, tables, out, track, along, total, near, filt, wave2, ready, finished):
     domains = fields.shape[0]
     bead_count = lax.axis_size("bead")
     device = lax.axis_index("grid") * bead_count + lax.axis_index("bead")
@@ -137,13 +138,32 @@
     group = lax.rem(device, groups)
     part = lax.div(device, groups)
     bins = GX // BIN
-    pack = min(2, domains)
-    unroll = min(8, domains) // pack
-    chunks = domains // (pack * unroll)
-
-    def block(first, where):
-        own = [fields[first + i, :, where] for i in range(pack)]
-        return jnp.concatenate(own, axis=1)
+    cells_all = GX * WAVES
+    halo = (WINDOW - BIN) * WAVES
+    pack = 2
+    packs = domains // pack
+    unroll = min(4, packs)
+    chunks = packs // unroll
+
+    for d in range(domains) if domains <= 8 else ():
+        for k, rows in enumerate(tracks(fields[d])):
+            track[d, k] = rows
+    if domains > 8:
+        def fill(d, carry):
+            for k, rows in enumerate(tracks(fields[d])):
+                track[d, k] = rows
+            return carry
+        lax.fori_loop(0, domains, fill, 0)
+
+    def rows_of(first, where, dim):
+        def one(k):
+            return jnp.concatenate(
+                [track[first + i, k, dim:dim + 1, where] for i in range(pack)], axis=1
+            )
+        return one(0).astype(jnp.int32), [one(1 + k) for k in range(4)], [one(5 + k) for k in range(4)]
+
+    def span(s):
+        return pl.ds(pl.multiple_of(s * CAP, CAP), CAP)
 
     row = lax.broadcasted_iota(jnp.int32, (GX, GZ), 0)
     col = lax.broadcasted_iota(jnp.int32, (GX, GZ), 1)
@@ -155,77 +175,135 @@
         times = jnp.where(lax.div(col * parts, GZ) == part, times, 0.0)
     wave2[...] = square
     filt[...] = times * jnp.exp(square * (-1.0 / (2.0 * screen_width * screen_width)))
-
-    for r in range(WAVES):
-        total[r, 0:GX + 8, :] = jnp.zeros((GX + 8, GZ), jnp.float32)
-
-    def spread(step, carry):
+    total[...] = jnp.zeros_like(total)
+    lanes = total.shape[2]
+    tiles = total.shape[0]
+
+    def load(rows):
+        return jnp.concatenate([total[i, rows, :] for i in range(tiles)], axis=1)
+
+    def store(rows, value):
+        for i in range(tiles):
+            total[i, rows, :] = value[:, i * lanes:(i + 1) * lanes]
+
+    def spread(i, carry):
+        for k in range(2):
+            spread_bin(2 * i + k)
+        return carry
+
+    def spread_bin(step):
         s = step // chunks
-        where = pl.ds(pl.multiple_of(s * CAP, CAP), CAP)
-        base = s * BIN
-        part_sum = None
+        where = span(s)
+        got = None
         for j in range(unroll):
-            own = block((step % chunks) * (unroll * pack) + j * pack, where)
-            x, = window(own[1:2], base, False)
-            y, = lines(own[2:3], group, False)
-            z, = stencil(own[3:4], GZ, False)
-            y = y * own[0:1]
-            rows = split(jnp.concatenate([x * y[r:r + 1] for r in range(WAVES)], axis=0))
-            got = dot3(rows, z, NT)
-            part_sum = got if part_sum is None else part_sum + got
-        rows = pl.ds(pl.multiple_of(base, 8), WINDOW)
-        for r in range(WAVES):
-            total[r, rows, :] += part_sum[r * WINDOW:(r + 1) * WINDOW]
+            pair = (step % chunks) * unroll + j
+            first = pair * pack
+            cells, values, _ = rows_of(first, where, 1)
+            x, = window(cells - s * BIN, [values])
+            cells, values, slopes = rows_of(first, where, 2)
+            y, yd = lines(cells, [values, slopes], group)
+            along[pair, s, 0] = y
+            along[pair, s, 1] = yd
+            charge = jnp.concatenate([fields[first + i, 0:1, where] for i in range(pack)], axis=1)
+            y = y * charge
+            cells, values, _ = rows_of(first, where, 3)
+            z, = stencil(cells, [values], GZ)
+            rows = split(jnp.concatenate([x[i:i + 1] * y for i in range(WINDOW)], axis=0))
+            more = dot3(rows, z, NT)
+            got = more if got is None else got + more
+        rows = pl.ds(pl.multiple_of(s * (BIN * WAVES), BIN * WAVES), WINDOW * WAVES)
+        store(rows, load(rows) + got)
+
+    lax.fori_loop(0, bins * chunks // 2, spread, 0)
+    total[:, 0:halo, :] += total[:, cells_all:cells_all + halo, :]
+    ready()
+
+    chains = 4
+    size = cells_all // (2 * chains)
+
+    def row_blocks(i):
+        return [pl.ds(pl.multiple_of((i * chains + k) * size, size), size) for k in range(chains)]
+
+    def forward(i, carry):
+        at = row_blocks(i)
+        got = [dot3(split(load(rows)), (rt[0], rt[1]), NN) for rows in at]
+        for rows, each in zip(at, got):
+            store(rows, each)
         return carry
-    lax.fori_loop(0, bins * chunks, spread, 0)
-
-    ready()
-
-    def transform(r, carry):
-        wave, _ = wave_of_row(group, r)
-        wave = jnp.full((1, GZ), wave, jnp.int32)
-        wave_square = (wave * wave).astype(jnp.float32)
-        count = jnp.where((wave & (GY // 2 - 1)) == 0, 1.0, 2.0)
-        scale = count * jnp.exp(wave_square * (-1.0 / (2.0 * screen_width * screen_width))) * (coulomb_scale / (GX * GY * GZ))
-        total[r, 0:8, :] += total[r, GX:GX + 8, :]
-        t = dot3((fx[0], fx[1]), split(total[r, 0:GX, :]), NN)
-        t = dot3(split(t), (rt[0], rt[1]), NN)
-        m2 = wave2[...] + wave_square
-        t = t * jnp.where(m2 == 0.0, 0.0, filt[...] * scale / jnp.where(m2 == 0.0, 1.0, m2))
-        t = dot3(split(t), (back[0], back[1]), NN)
-        t = dot3((fxt[0], fxt[1]), split(t), NN)
-        total[r, 0:GX, :] = t
-        total[r, GX:GX + 8, :] = t[0:8]
+
+    lax.fori_loop(0, 2, forward, 0)
+
+    def middle(i, carry):
+        at = [pl.ds(i * chains + k, GX, stride=WAVES) for k in range(chains)]
+        got = [dot3((fx[0], fx[1]), split(load(rows)), NN) for rows in at]
+        for k in range(chains):
+            wave, _ = wave_of_row(group, i * chains + k)
+            wave = jnp.full((1, GZ), wave, jnp.int32)
+            wave_square = (wave * wave).astype(jnp.float32)
+            count = jnp.where((wave & (GY // 2 - 1)) == 0, 1.0, 2.0)
+            scale = count * jnp.exp(wave_square * (-1.0 / (2.0 * screen_width * screen_width)))
+            scale = scale * (coulomb_scale / (GX * GY * GZ))
+            m2 = wave2[...] + wave_square
+            got[k] = got[k] * jnp.where(m2 == 0.0, 0.0, filt[...] * scale / jnp.where(m2 == 0.0, 1.0, m2))
+        got = [dot3((fxt[0], fxt[1]), split(each), NN) for each in got]
+        for rows, each in zip(at, got):
+            store(rows, each)
         return carry
-    lax.fori_loop(0, WAVES, transform, 0)
+
+    lax.fori_loop(0, WAVES // chains, middle, 0)
+
+    def inverse(i, carry):
+        at = row_blocks(i)
+        got = [dot3(split(load(rows)), (back[0], back[1]), NN) for rows in at]
+        for rows, each in zip(at, got):
+            high, low = split(each)
+            near[0, rows, :] = high
+            near[1, rows, :] = low
+        return carry
+
+    lax.fori_loop(0, 2, inverse, 0)
+    near[:, cells_all:cells_all + halo, :] = near[:, 0:halo, :]
+
+    half = min(8, bins)
+    own_pack = lax.axis_index("grid") // pack
 
     def gather(step, carry):
-        s = step // chunks
-        where = pl.ds(pl.multiple_of(s * CAP, CAP), CAP)
-        base = s * BIN
-        rows = pl.ds(pl.multiple_of(base, 8), WINDOW)
-        near = split(jnp.concatenate([total[r, rows, :] for r in range(WAVES)], axis=0))
-        for j in range(unroll):
-            first = (step % chunks) * (unroll * pack) + j * pack
-            own = block(first, where)
-            x, xd = window(own[1:2], base, True)
-            y, yd = lines(own[2:3], group, True)
-            z, zd = stencil(own[3:4], GZ, True)
-            plain = dot3(near, z, NN)
-            steep = dot3(near, zd, NN)
+        pair = lax.rem(own_pack + 1 + step // (bins // half), packs)
+        first = pair * pack
+        for j in range(half):
+            s = (step % (bins // half)) * half + j
+            where = span(s)
+            rows = pl.ds(pl.multiple_of(s * (BIN * WAVES), BIN * WAVES), WINDOW * WAVES)
+            field = (near[0, rows, :], near[1, rows, :])
+            cells, values, slopes = rows_of(first, where, 1)
+            x, xd = window(cells - s * BIN, [values, slopes])
+            cells, values, slopes = rows_of(first, where, 3)
+            z, zd = stencil(cells, [values, slopes], GZ)
+            plain = dot3(field, z, NN)
+            steep = dot3(field, zd, NN)
             f = [0.0, 0.0, 0.0]
-            for r in range(WAVES):
-                q = plain[r * WINDOW:(r + 1) * WINDOW]
-                f[0] = f[0] + q * y[r:r + 1]
-                f[1] = f[1] + q * yd[r:r + 1]
-                f[2] = f[2] + steep[r * WINDOW:(r + 1) * WINDOW] * y[r:r + 1]
-            f = [f[0] * xd, f[1] * x, f[2] * x]
+            for i in range(WINDOW):
+                q = plain[i * WAVES:(i + 1) * WAVES]
+                f[0] = f[0] + q * xd[i:i + 1]
+                f[1] = f[1] + q * x[i:i + 1]
+                f[2] = f[2] + steep[i * WAVES:(i + 1) * WAVES] * x[i:i + 1]
+            y, yd = along[pair, s, 0], along[pair, s, 1]
+            f = [f[0] * y, f[1] * yd, f[2] * y]
+            charge = jnp.concatenate([fields[first + i, 0:1, where] for i in range(pack)], axis=1)
             for c in range(3):
-                force = -own[0:1] * jnp.sum(f[c], axis=0, keepdims=True)
+                force = -charge * jnp.sum(f[c], axis=0, keepdims=True)
                 for i in range(pack):
                     out[first + i, c:c + 1, where] = force[:, i * CAP:(i + 1) * CAP]
+
+        @pl.when(step % (bins // half) == bins // half - 1)
+        def _():
+            for i in range(pack):
+                finished(first + i)
+
         return carry
-    lax.fori_loop(0, bins * chunks, gather, 0)
+
+    lax.fori_loop(0, packs * (bins // half), gather, 0)
+
 
 def wave_of_row(group, row):
     half = WAVES // 2
@@ -272,7 +350,9 @@
     me = lax.axis_index(name)
 
     def copy(step, landing):
-        peer = lax.rem(me + step, count)
+        return send(lax.rem(me + step, count), landing)
+
+    def send(peer, landing):
         return pltpu.make_async_remote_copy(
             src_ref=source(peer),
             dst_ref=target(peer if landing else me),
@@ -303,7 +383,7 @@
 
         lax.fori_loop(1, count, one, 0)
 
-    return start, wait, drain
+    return start, wait, drain, lambda peer: send(peer, False).start()
 
 
 def split3(value):
@@ -408,7 +488,7 @@
     planes, centre, neighbours, positions, momenta, noise, charges, route, cells, offsets, mixing, waves,
     new_positions, new_momenta,
     own_momenta, own_charges, own_route, own_cells, own_offsets, own_mixing, own_waves,
-    fields, sources, kicks, partial, landed, level, last, total, filt, wave2,
+    fields, sources, kicks, partial, landed, level, last, track, along, total, near, filt, wave2,
     local_sem, field_send, field_recv, place_send, place_recv, noise_send, noise_recv,
     kick_send, kick_recv, part_send, part_recv, last_send, last_recv,
 ):
@@ -461,8 +541,14 @@
     kick[0]()
     field[1]()
 
-    mesh_phases(fields, own_waves, partial, total, filt, wave2, loads[8].wait)
-    part[0]()
+    def finished(d):
+        @pl.when(d != grid_rank)
+        def _():
+            part[3](d)
+
+    mesh_phases(
+        fields, own_waves, partial, track, along, total, near, filt, wave2, loads[8].wait, finished
+    )
 
     landed[grid_rank] = partial[grid_rank]
     where = placement(slot)
@@ -537,7 +623,10 @@
             f32(grid_count, 3, slots),
             f32(3, slots),
             f32(bead_count, 3, slots),
-            f32(WAVES, GX + 8, GZ),
+            f32(grid_count, 9, 4, slots),
+            f32(grid_count // 2, GX // BIN, 2, WAVES, 2 * CAP),
+            f32(GZ // 128, (GX + WINDOW - BIN) * WAVES, 128),
+            pltpu.VMEM((2, (GX + WINDOW - BIN) * WAVES, GZ), jnp.bfloat16),
             f32(GX, GZ),
             f32(GX, GZ),
             dma((9,)),

time: 56.9 us -> 47.6 us (0.84)
  Pallas kernels: 53.9 us -> 44.7 us
    pallas_call x1, Pallas kernels: 53.9 us -> 44.7 us  [per_device(): pl.pallas_call(functools.partial(step_kernel, GX // grid_count, centre),...]
where the time goes in v3:
time: 47.6 us; the launch traced here: 47.4 us
  Pallas kernels  44.7 us (94%)
  local copies, waits for them, and re-layouts  2.06 us (4%)
  between operations  0.65 us (1%)
    pallas_call x1, Pallas kernels, per_device(): pl.pallas_call(functools.partial(step_kernel, GX // grid_count, centre),...  44.7 us
    unnamed x4, local copies, waits for them, and re-layouts  2.06 us

profile of v3, /device:TPU:0, one launch (start us, length us, event | category | flops | bytes accessed | tf_op | source)
XLA Modules:
  0.0 47.4 jit_solution(18424686275518183877)
XLA Ops:
  0.6 44.7 %shard_map.176 = (f32[3,8,512]{2,1,0:T(8,128)}, f32[3,8,512]{2,1,0:T(8,128)}) custom-call(s32[4,4]{1,0:T(4,128)} %neighbours.1, f32[3,8,512]{2,1,0:T(8,128)} %positions.1, f32[3,8,512]{2,1,0:T(8,128)} %momenta.1, f32[3,8,512]{2,1,0:T(8,128)} %noise.1, f32[1,512]{1,0:T(1,128)} %bitcast.2, s32[1,512]{1,0:T(1,128)} %bitcast.3, s32[3,512]{1,0:T(4,128)} %cells.1, ...), custom_call_target="tpu_custom_call" | custom-call | tf_op jit(solution)/shard_map/pallas_call | solution.py:611
  45.3 0.0 copy-start
  45.3 1.4 %copy.21 = f32[3,8,512]{2,1,0:T(8,128)} copy(f32[3,8,512]{2,1,0:T(8,128)} %get-tuple-element.4) | data formatting | bytes 98304
  46.8 0.0 copy-done
  46.8 0.6 %copy.22 = f32[3,8,512]{2,1,0:T(8,128)} copy(f32[3,8,512]{2,1,0:T(8,128)S(1)} %copy-done) | data formatting | bytes 98304
Async XLA Ops:
  45.3 1.4 %copy-start = (f32[3,8,512]{2,1,0:T(8,128)S(1)}, f32[3,8,512]{2,1,0:T(8,128)}, u32[]{:S(2)}) copy-start(f32[3,8,512]{2,1,0:T(8,128)} %get-tuple-element.5) | copy-start | bytes 147460

commit v4 on v3

--- a/solution.py
+++ b/solution.py
@@ -128,15 +128,34 @@
     return found
 
 
-def mesh_phases(fields, tables, out, track, along, total, near, filt, wave2, ready, finished):
+def mesh_filter(total, filt):
+    bead_count = lax.axis_size("bead")
+    device = lax.axis_index("grid") * bead_count + lax.axis_index("bead")
+    groups = GY // WAVES
+    parts = lax.axis_size("grid") * bead_count // groups
+    group = lax.rem(device, groups)
+    part = lax.div(device, groups)
+    reach = -1.0 / (2.0 * screen_width * screen_width)
+    row = lax.broadcasted_iota(jnp.int32, (GX, GZ), 0)
+    col = lax.broadcasted_iota(jnp.int32, (GX, GZ), 1)
+    wx = jnp.where(row <= GX // 2, row, row - GX // 2)
+    wz = jnp.where(col <= GZ // 2, col, col - GZ // 2)
+    square = (wx * wx + wz * wz).astype(jnp.float32)
+    times = jnp.where((wx & (GX // 2 - 1)) == 0, 1.0, 2.0) * jnp.where((wz & (GZ // 2 - 1)) == 0, 1.0, 2.0)
+    if parts > 1:
+        times = jnp.where(lax.div(col * parts, GZ) == part, times, 0.0)
+    plain = times * jnp.exp(square * reach)
+    filt[0] = plain
+    filt[1] = square
+    total[...] = jnp.zeros_like(total)
+
+
+def mesh_phases(fields, tables, out, track, along, total, near, filt, ready, finished):
     domains = fields.shape[0]
     bead_count = lax.axis_size("bead")
     device = lax.axis_index("grid") * bead_count + lax.axis_index("bead")
     fx, fxt, rt, back = [tables.at[i] for i in range(4)]
-    groups = GY // WAVES
-    parts = lax.axis_size("grid") * bead_count // groups
-    group = lax.rem(device, groups)
-    part = lax.div(device, groups)
+    group = lax.rem(device, GY // WAVES)
     bins = GX // BIN
     cells_all = GX * WAVES
     halo = (WINDOW - BIN) * WAVES
@@ -165,17 +184,6 @@
     def span(s):
         return pl.ds(pl.multiple_of(s * CAP, CAP), CAP)
 
-    row = lax.broadcasted_iota(jnp.int32, (GX, GZ), 0)
-    col = lax.broadcasted_iota(jnp.int32, (GX, GZ), 1)
-    wx = jnp.where(row <= GX // 2, row, row - GX // 2)
-    wz = jnp.where(col <= GZ // 2, col, col - GZ // 2)
-    square = (wx * wx + wz * wz).astype(jnp.float32)
-    times = jnp.where((wx & (GX // 2 - 1)) == 0, 1.0, 2.0) * jnp.where((wz & (GZ // 2 - 1)) == 0, 1.0, 2.0)
-    if parts > 1:
-        times = jnp.where(lax.div(col * parts, GZ) == part, times, 0.0)
-    wave2[...] = square
-    filt[...] = times * jnp.exp(square * (-1.0 / (2.0 * screen_width * screen_width)))
-    total[...] = jnp.zeros_like(total)
     lanes = total.shape[2]
     tiles = total.shape[0]
 
@@ -187,8 +195,8 @@
             total[i, rows, :] = value[:, i * lanes:(i + 1) * lanes]
 
     def spread(i, carry):
-        for k in range(2):
-            spread_bin(2 * i + k)
+        for k in range(4):
+            spread_bin(4 * i + k)
         return carry
 
     def spread_bin(step):
@@ -214,12 +222,12 @@
         rows = pl.ds(pl.multiple_of(s * (BIN * WAVES), BIN * WAVES), WINDOW * WAVES)
         store(rows, load(rows) + got)
 
-    lax.fori_loop(0, bins * chunks // 2, spread, 0)
+    lax.fori_loop(0, bins * chunks // 4, spread, 0)
     total[:, 0:halo, :] += total[:, cells_all:cells_all + halo, :]
     ready()
 
-    chains = 4
-    size = cells_all // (2 * chains)
+    chains = WAVES
+    size = cells_all // chains
 
     def row_blocks(i):
         return [pl.ds(pl.multiple_of((i * chains + k) * size, size), size) for k in range(chains)]
@@ -231,7 +239,7 @@
             store(rows, each)
         return carry
 
-    lax.fori_loop(0, 2, forward, 0)
+    forward(0, 0)
 
     def middle(i, carry):
         at = [pl.ds(i * chains + k, GX, stride=WAVES) for k in range(chains)]
@@ -243,14 +251,14 @@
             count = jnp.where((wave & (GY // 2 - 1)) == 0, 1.0, 2.0)
             scale = count * jnp.exp(wave_square * (-1.0 / (2.0 * screen_width * screen_width)))
             scale = scale * (coulomb_scale / (GX * GY * GZ))
-            m2 = wave2[...] + wave_square
-            got[k] = got[k] * jnp.where(m2 == 0.0, 0.0, filt[...] * scale / jnp.where(m2 == 0.0, 1.0, m2))
+            m2 = filt[1] + wave_square
+            got[k] = got[k] * jnp.where(m2 == 0.0, 0.0, filt[0] * scale / jnp.where(m2 == 0.0, 1.0, m2))
         got = [dot3((fxt[0], fxt[1]), split(each), NN) for each in got]
         for rows, each in zip(at, got):
             store(rows, each)
         return carry
 
-    lax.fori_loop(0, WAVES // chains, middle, 0)
+    middle(0, 0)
 
     def inverse(i, carry):
         at = row_blocks(i)
@@ -261,7 +269,7 @@
             near[1, rows, :] = low
         return carry
 
-    lax.fori_loop(0, 2, inverse, 0)
+    inverse(0, 0)
     near[:, cells_all:cells_all + halo, :] = near[:, 0:halo, :]
 
     half = min(8, bins)
@@ -328,21 +336,26 @@
 MESH = pl.DeviceIdType.MESH
 
 
-def greet(names):
+def everyone(act):
+    grid_count, bead_count = lax.axis_size("grid"), lax.axis_size("bead")
+    me = lax.axis_index("grid") * bead_count + lax.axis_index("bead")
+
+    def one(step, carry):
+        peer = lax.rem(me + step, grid_count * bead_count)
+        act(lax.div(peer, bead_count), lax.rem(peer, bead_count))
+        return carry
+
+    lax.fori_loop(1, grid_count * bead_count, one, 0)
+    return grid_count * bead_count - 1
+
+
+def hail():
     barrier = pltpu.get_barrier_semaphore()
-    total = 0
-    for name in names:
-        count = lax.axis_size(name)
-        me = lax.axis_index(name)
-
-        def signal(step, carry):
-            peer = lax.rem(me + step, count)
-            pl.semaphore_signal(barrier, 1, device_id={name: peer}, device_id_type=MESH)
-            return carry
-
-        lax.fori_loop(1, count, signal, 0)
-        total += count - 1
-    pl.semaphore_wait(barrier, total)
+
+    def signal(g, b):
+        pl.semaphore_signal(barrier, 1, device_id=(g, b), device_id_type=MESH)
+
+    return everyone(signal)
 
 
 def shares(name, source, target, send_sem, recv_sem):
@@ -350,9 +363,7 @@
     me = lax.axis_index(name)
 
     def copy(step, landing):
-        return send(lax.rem(me + step, count), landing)
-
-    def send(peer, landing):
+        peer = lax.rem(me + step, count)
         return pltpu.make_async_remote_copy(
             src_ref=source(peer),
             dst_ref=target(peer if landing else me),
@@ -383,7 +394,7 @@
 
         lax.fori_loop(1, count, one, 0)
 
-    return start, wait, drain, lambda peer: send(peer, False).start()
+    return start, wait, drain
 
 
 def split3(value):
@@ -486,11 +497,11 @@
 
 def step_kernel(
     planes, centre, neighbours, positions, momenta, noise, charges, route, cells, offsets, mixing, waves,
-    new_positions, new_momenta,
+    drifted, force_q, force_p,
     own_momenta, own_charges, own_route, own_cells, own_offsets, own_mixing, own_waves,
-    fields, sources, kicks, partial, landed, level, last, track, along, total, near, filt, wave2,
+    fields, sources, kicks, partial, landed, steps, track, along, total, near, filt,
     local_sem, field_send, field_recv, place_send, place_recv, noise_send, noise_recv,
-    kick_send, kick_recv, part_send, part_recv, last_send, last_recv,
+    kick_send, kick_recv, part_send, part_recv,
 ):
     grid_rank = lax.axis_index("grid")
     bead_rank = lax.axis_index("bead")
@@ -498,6 +509,7 @@
     domains = partial.shape[0]
     beads = kicks.shape[2]
 
+    others = hail()
     pairs = [
         (route, own_route), (charges, own_charges), (cells, own_cells), (offsets, own_offsets),
         (positions, sources.at[bead_rank, 0]), (momenta, own_momenta),
@@ -514,20 +526,31 @@
     first = (rows * planes + own_cells[0:1]).astype(jnp.float32) + own_offsets[0:1]
     rest = own_cells[1:3].astype(jnp.float32) + own_offsets[1:3]
     own = jnp.concatenate([own_charges[...], first, rest], axis=0)
-    halves = [part.astype(jnp.float32) for part in split3(own)]
+    halves = [each.astype(jnp.float32) for each in split3(own)]
     packed = jnp.concatenate(halves + [jnp.zeros_like(own)], axis=0).astype(jnp.bfloat16)
     got = lax.dot_general(packed, placement(slot), (NT, ((), ())), preferred_element_type=jnp.float32)
     fields[grid_rank] = (got[0:4] + got[4:8]) + got[8:12]
 
-    greet(("grid", "bead"))
+    pl.semaphore_wait(pltpu.get_barrier_semaphore(), others)
     field = shares("grid", lambda p: fields.at[grid_rank], lambda p: fields.at[p], field_send, field_recv)
     place = shares("bead", lambda p: positions, lambda p: sources.at[p, 0], place_send, place_recv)
     draw = shares("bead", lambda p: noise, lambda p: sources.at[p, 1], noise_send, noise_recv)
     kick = shares("bead", lambda p: kicks.at[bead_rank], lambda p: kicks.at[p], kick_send, kick_recv)
-    part = shares("grid", lambda p: partial.at[p], lambda p: landed.at[p], part_send, part_recv)
-    summed = shares("bead", lambda p: level, lambda p: last.at[p], last_send, last_recv)
+
+    def part(g, b, landing=False):
+        return pltpu.make_async_remote_copy(
+            src_ref=partial.at[g],
+            dst_ref=landed.at[g, b] if landing else landed.at[grid_rank, bead_rank],
+            send_sem=part_send.at[g, b],
+            recv_sem=part_recv.at[g, b] if landing else part_recv.at[grid_rank, bead_rank],
+            device_id=(g, b),
+            device_id_type=MESH,
+        )
+
     for each in (field, place, draw):
         each[0]()
+
+    mesh_filter(total, filt)
 
     def weight_of(t, m):
         total = 0.0
@@ -542,15 +565,18 @@
     field[1]()
 
     def finished(d):
-        @pl.when(d != grid_rank)
-        def _():
-            part[3](d)
+        for k in range(bead_count):
+            mate = lax.rem(bead_rank + 1 + k, bead_count)
+
+            @pl.when((d != grid_rank) | (mate != bead_rank))
+            def _():
+                part(d, mate).start()
 
     mesh_phases(
-        fields, own_waves, partial, track, along, total, near, filt, wave2, loads[8].wait, finished
+        fields, own_waves, partial, track, along, total, near, filt, loads[8].wait, finished
     )
 
-    landed[grid_rank] = partial[grid_rank]
+    landed[grid_rank, bead_rank] = partial[grid_rank]
     where = placement(slot)
     for each in (place, draw, kick):
         each[1]()
@@ -563,32 +589,35 @@
         parts += [kicks[k, c] for k in range(bead_count)]
         parts += [sources[k, 1, c] for k in range(bead_count)]
         got = jnp.dot(mix, jnp.concatenate(parts, axis=0), precision=highest, preferred_element_type=jnp.float32)
-        new_positions[c] = got[0:beads]
-        new_momenta[c] = got[beads:]
-
-    stepped(0)
-    part[1]()
-    forces = landed[0]
-    for d in range(1, domains):
-        forces = forces + landed[d]
-    level[...] = forces
-    last[bead_rank] = forces
-    summed[0]()
-    stepped(1)
-    stepped(2)
-    summed[1]()
-    forces = last[0]
-    for k in range(1, bead_count):
-        forces = forces + last[k]
-    halves = [part.astype(jnp.float32) for part in split3(forces)]
+        steps[0, c] = got[0:beads]
+        steps[1, c] = got[beads:]
+
+    for component in range(3):
+        stepped(component)
+    leave = pltpu.make_async_copy(steps, drifted, local_sem.at[len(pairs)])
+    leave.start()
+    everyone(lambda g, b: part(g, b, True).wait_recv())
+    forces = jnp.zeros(partial.shape[1:], jnp.float32)
+    if domains <= 8:
+        for d in range(domains):
+            for k in range(bead_count):
+                forces = forces + landed[d, k]
+    else:
+        def add(d, forces):
+            for k in range(bead_count):
+                forces = forces + landed[d, k]
+            return forces
+        forces = lax.fori_loop(0, domains, add, forces)
+    halves = [each.astype(jnp.float32) for each in split3(forces)]
     packed = jnp.concatenate(halves + [jnp.zeros((16 - 9, forces.shape[1]), jnp.float32)], axis=0)
     got = jnp.dot(packed.astype(jnp.bfloat16), where, preferred_element_type=jnp.float32)
     force = (got[0:3] + got[3:6]) + got[6:9]
-    for c in range(3):
-        new_positions[c] += centre[0] * force[c : c + 1]
-        new_momenta[c] += centre[1] * force[c : c + 1]
-    for each in (field, place, draw, kick, part, summed):
+    force_q[...] = centre[0] * force
+    force_p[...] = centre[1] * force
+    leave.wait()
+    for each in (field, place, draw, kick):
         each[2]()
+    everyone(lambda g, b: part(g, b).wait_send())
 
 
 def per_device(positions, momenta, noise, charges, slab_route, cells, offsets, nbr_tiles):
@@ -608,11 +637,15 @@
     f32 = lambda *shape: pltpu.VMEM(shape, jnp.float32)
     charges = charges.reshape(1, atoms)
     slab_route = slab_route.reshape(1, atoms)
-    return pl.pallas_call(
+    drifted, *force = pl.pallas_call(
         functools.partial(step_kernel, GX // grid_count, centre),
-        out_shape=[jax.ShapeDtypeStruct(positions.shape, jnp.float32)] * 2,
+        out_shape=[
+            jax.ShapeDtypeStruct((2, *positions.shape), jnp.float32),
+            jax.ShapeDtypeStruct((3, atoms), jnp.float32),
+            jax.ShapeDtypeStruct((3, atoms), jnp.float32),
+        ],
         in_specs=[pl.BlockSpec(memory_space=pltpu.SMEM)] + [anywhere] * 9,
-        out_specs=[vmem] * 2,
+        out_specs=[anywhere, vmem, vmem],
         scratch_shapes=[
             whole(momenta), whole(charges), whole(slab_route), whole(cells), whole(offsets),
             whole(shaped), whole(waves),
@@ -620,25 +653,23 @@
             f32(bead_count, 2, *positions.shape),
             f32(bead_count, *positions.shape),
             f32(grid_count, 3, slots),
-            f32(grid_count, 3, slots),
-            f32(3, slots),
-            f32(bead_count, 3, slots),
+            f32(grid_count, bead_count, 3, slots),
+            f32(2, *positions.shape),
             f32(grid_count, 9, 4, slots),
             f32(grid_count // 2, GX // BIN, 2, WAVES, 2 * CAP),
             f32(GZ // 128, (GX + WINDOW - BIN) * WAVES, 128),
             pltpu.VMEM((2, (GX + WINDOW - BIN) * WAVES, GZ), jnp.bfloat16),
-            f32(GX, GZ),
-            f32(GX, GZ),
-            dma((9,)),
+            f32(2, GX, GZ),
+            dma((10,)),
             dma((grid_count,)), dma((grid_count,)),
             *[dma((bead_count,)) for _ in range(6)],
-            dma((grid_count,)), dma((grid_count,)),
-            *[dma((bead_count,)) for _ in range(2)],
+            dma((grid_count, bead_count)), dma((grid_count, bead_count)),
         ],
         compiler_params=pltpu.CompilerParams(
             collective_id=0, has_side_effects=True, vmem_limit_bytes=60 * 1024 * 1024
         ),
     )(nbr_tiles, positions, momenta, noise, charges, slab_route, cells, offsets, shaped, waves)
+    return tuple(drifted[i] + force[i][:, None, :] for i in range(2))
 
 
 def solution(mesh):

time: 47.6 us -> 44.7 us (0.939)
  Pallas kernels: 44.7 us -> 42.3 us
  local copies, waits for them, and re-layouts: 2.06 us -> 0 us
  other arithmetic: 0 us -> 1.47 us
    pallas_call x1, Pallas kernels: 44.7 us -> 42.3 us  [per_device(): pl.pallas_call(functools.partial(step_kernel, GX // grid_count, centre),...]
    unnamed x4 -> x0, local copies, waits for them, and re-layouts: 2.06 us -> none
    add x0 -> x1, other arithmetic: none -> 1.47 us  [per_device(): return tuple((drifted[i] + force[i][:, None, :] for i in range(2)))]
where the time goes in v4:
time: 44.7 us; the launch traced here: 44.5 us
  Pallas kernels  42.3 us (95%)
  other arithmetic  1.47 us (3%)
  between operations  0.64 us (1%)
    pallas_call x1, Pallas kernels, per_device(): pl.pallas_call(functools.partial(step_kernel, GX // grid_count, centre),...  42.3 us
    add x1, other arithmetic, per_device(): return tuple((drifted[i] + force[i][:, None, :] for i in range(2)))  1.47 us

profile of v4, /device:TPU:0, one launch (start us, length us, event | category | flops | bytes accessed | tf_op | source)
XLA Modules:
  0.0 44.5 jit_solution(2462174443486750935)
XLA Ops:
  0.6 42.3 %shard_map.176 = (f32[2,3,8,512]{3,2,1,0:T(8,128)}, f32[3,512]{1,0:T(4,128)}, f32[3,512]{1,0:T(4,128)}) custom-call(s32[4,4]{1,0:T(4,128)} %neighbours.1, f32[3,8,512]{2,1,0:T(8,128)} %positions.1, f32[3,8,512]{2,1,0:T(8,128)} %momenta.1, f32[3,8,512]{2,1,0:T(8,128)} %noise.1, f32[1,512]{1,0:T(1,128)} %bitcast.6, s32[1,512]{1,0:T(1,128)} %bitcast.7, ...), custom_call_target="tpu_custom_call" | custom-call | tf_op jit(solution)/shard_map/pallas_call | solution.py:640
  43.0 1.5 %bitcast_add_fusion = (f32[3,8,512]{2,1,0:T(8,128)}, f32[3,8,512]{2,1,0:T(8,128)}) fusion(f32[2,3,8,512]{3,2,1,0:T(8,128)} %get-tuple-element.5, f32[3,512]{1,0:T(4,128)} %get-tuple-element.7, f32[3,512]{1,0:T(4,128)} %get-tuple-element.6), kind=kLoop, calls=%fused_computation | loop fusion | flops 24576 | bytes 208896 | tf_op jit(solution)/shard_map/add | solution.py:672

commit v5 on v4

--- a/solution.py
+++ b/solution.py
@@ -14,6 +14,7 @@
 BIN = 32
 WINDOW = 36
 CAP = 128
+PACK = 2
 coulomb_scale = 100000.0
 screen_width = 200.0
 
@@ -159,7 +160,7 @@
     bins = GX // BIN
     cells_all = GX * WAVES
     halo = (WINDOW - BIN) * WAVES
-    pack = 2
+    pack = PACK
     packs = domains // pack
     unroll = min(4, packs)
     chunks = packs // unroll
@@ -301,12 +302,11 @@
             for c in range(3):
                 force = -charge * jnp.sum(f[c], axis=0, keepdims=True)
                 for i in range(pack):
-                    out[first + i, c:c + 1, where] = force[:, i * CAP:(i + 1) * CAP]
+                    out[first + i, pl.ds(c * bins + s, 1), :] = force[:, i * CAP:(i + 1) * CAP]
 
         @pl.when(step % (bins // half) == bins // half - 1)
         def _():
-            for i in range(pack):
-                finished(first + i)
+            finished(pair)
 
         return carry
 
@@ -499,9 +499,9 @@
     planes, centre, neighbours, positions, momenta, noise, charges, route, cells, offsets, mixing, waves,
     drifted, force_q, force_p,
     own_momenta, own_charges, own_route, own_cells, own_offsets, own_mixing, own_waves,
-    fields, sources, kicks, partial, landed, steps, track, along, total, near, filt,
+    fields, sources, kicks, partial, landed, mates, level, last, steps, track, along, total, near, filt,
     local_sem, field_send, field_recv, place_send, place_recv, noise_send, noise_recv,
-    kick_send, kick_recv, part_send, part_recv,
+    kick_send, kick_recv, part_send, part_recv, mate_send, mate_recv, last_send, last_recv,
 ):
     grid_rank = lax.axis_index("grid")
     bead_rank = lax.axis_index("bead")
@@ -536,16 +536,46 @@
     place = shares("bead", lambda p: positions, lambda p: sources.at[p, 0], place_send, place_recv)
     draw = shares("bead", lambda p: noise, lambda p: sources.at[p, 1], noise_send, noise_recv)
     kick = shares("bead", lambda p: kicks.at[bead_rank], lambda p: kicks.at[p], kick_send, kick_recv)
-
-    def part(g, b, landing=False):
+    summed = shares("bead", lambda p: level, lambda p: last.at[p], last_send, last_recv)
+    own_pack = lax.div(grid_rank, PACK)
+    place_in = lax.rem(grid_rank, PACK)
+
+    def far(g, landing=False):
         return pltpu.make_async_remote_copy(
             src_ref=partial.at[g],
-            dst_ref=landed.at[g, b] if landing else landed.at[grid_rank, bead_rank],
-            send_sem=part_send.at[g, b],
-            recv_sem=part_recv.at[g, b] if landing else part_recv.at[grid_rank, bead_rank],
-            device_id=(g, b),
+            dst_ref=landed.at[g if landing else grid_rank],
+            send_sem=part_send.at[g],
+            recv_sem=part_recv.at[g if landing else grid_rank],
+            device_id={"grid": g},
             device_id_type=MESH,
         )
+
+    def close(step, landing=False):
+        peer = lax.rem(place_in * bead_count + bead_rank + step, PACK * bead_count)
+        i, b = lax.div(peer, bead_count), lax.rem(peer, bead_count)
+        at = (i, b) if landing else (place_in, bead_rank)
+        return pltpu.make_async_remote_copy(
+            src_ref=partial.at[own_pack * PACK + i],
+            dst_ref=mates.at[at],
+            send_sem=mate_send.at[i, b],
+            recv_sem=mate_recv.at[at],
+            device_id=(own_pack * PACK + i, b),
+            device_id_type=MESH,
+        )
+
+    def each_far(act):
+        def one(step, carry):
+            act(lax.rem((own_pack + 1) * PACK + step, domains))
+            return carry
+
+        lax.fori_loop(0, domains - PACK, one, 0)
+
+    def each_close(act):
+        def one(step, carry):
+            act(step)
+            return carry
+
+        lax.fori_loop(1, PACK * bead_count, one, 0)
 
     for each in (field, place, draw):
         each[0]()
@@ -564,19 +594,28 @@
     kick[0]()
     field[1]()
 
-    def finished(d):
-        for k in range(bead_count):
-            mate = lax.rem(bead_rank + 1 + k, bead_count)
-
-            @pl.when((d != grid_rank) | (mate != bead_rank))
-            def _():
-                part(d, mate).start()
+    def finished(pair):
+        @pl.when(pair != own_pack)
+        def _():
+            for i in range(PACK):
+                far(pair * PACK + i).start()
+
+        @pl.when(pair == own_pack)
+        def _():
+            each_close(lambda step: close(step).start())
 
     mesh_phases(
         fields, own_waves, partial, track, along, total, near, filt, loads[8].wait, finished
     )
 
-    landed[grid_rank, bead_rank] = partial[grid_rank]
+    mates[place_in, bead_rank] = partial[grid_rank]
+    each_far(lambda g: far(g, True).wait_recv())
+
+    def add(step, forces):
+        return forces + landed[lax.rem((own_pack + 1) * PACK + step, domains)]
+
+    level[...] = lax.fori_loop(0, domains - PACK, add, jnp.zeros(level.shape, jnp.float32))
+    summed[0]()
     where = placement(slot)
     for each in (place, draw, kick):
         each[1]()
@@ -596,18 +635,23 @@
         stepped(component)
     leave = pltpu.make_async_copy(steps, drifted, local_sem.at[len(pairs)])
     leave.start()
-    everyone(lambda g, b: part(g, b, True).wait_recv())
-    forces = jnp.zeros(partial.shape[1:], jnp.float32)
-    if domains <= 8:
-        for d in range(domains):
-            for k in range(bead_count):
-                forces = forces + landed[d, k]
-    else:
-        def add(d, forces):
-            for k in range(bead_count):
-                forces = forces + landed[d, k]
-            return forces
-        forces = lax.fori_loop(0, domains, add, forces)
+    each_close(lambda step: close(step, True).wait_recv())
+    forces = level[...]
+    for k in range(bead_count):
+        for i in range(PACK):
+            forces = forces + mates[i, k]
+    summed[1]()
+    last[bead_rank] = jnp.zeros(level.shape, jnp.float32)
+    for k in range(bead_count):
+        forces = forces + last[k]
+    bins = GX // BIN
+    forces = jnp.concatenate(
+        [
+            jnp.concatenate([forces[c * bins + s : c * bins + s + 1] for s in range(bins)], axis=1)
+            for c in range(3)
+        ],
+        axis=0,
+    )
     halves = [each.astype(jnp.float32) for each in split3(forces)]
     packed = jnp.concatenate(halves + [jnp.zeros((16 - 9, forces.shape[1]), jnp.float32)], axis=0)
     got = jnp.dot(packed.astype(jnp.bfloat16), where, preferred_element_type=jnp.float32)
@@ -615,9 +659,10 @@
     force_q[...] = centre[0] * force
     force_p[...] = centre[1] * force
     leave.wait()
-    for each in (field, place, draw, kick):
+    for each in (field, place, draw, kick, summed):
         each[2]()
-    everyone(lambda g, b: part(g, b).wait_send())
+    each_far(lambda g: far(g).wait_send())
+    each_close(lambda step: close(step).wait_send())
 
 
 def per_device(positions, momenta, noise, charges, slab_route, cells, offsets, nbr_tiles):
@@ -625,6 +670,7 @@
     bead_count = lax.axis_size("bead")
     beads, atoms = positions.shape[1:]
     slots = GX // BIN * CAP
+    sheet = (3 * (GX // BIN), CAP)
     tables, centre = step_tables(beads * bead_count)
     shaped = tables.reshape(2, 3, bead_count, beads, -1).transpose(2, 0, 3, 1, 4)
     shaped = jnp.asarray(shaped.reshape(bead_count, 2 * beads, -1))
@@ -652,8 +698,11 @@
             f32(grid_count, 4, slots),
             f32(bead_count, 2, *positions.shape),
             f32(bead_count, *positions.shape),
-            f32(grid_count, 3, slots),
-            f32(grid_count, bead_count, 3, slots),
+            f32(grid_count, *sheet),
+            f32(grid_count, *sheet),
+            f32(PACK, bead_count, *sheet),
+            f32(*sheet),
+            f32(bead_count, *sheet),
             f32(2, *positions.shape),
             f32(grid_count, 9, 4, slots),
             f32(grid_count // 2, GX // BIN, 2, WAVES, 2 * CAP),
@@ -663,7 +712,9 @@
             dma((10,)),
             dma((grid_count,)), dma((grid_count,)),
             *[dma((bead_count,)) for _ in range(6)],
-            dma((grid_count, bead_count)), dma((grid_count, bead_count)),
+            dma((grid_count,)), dma((grid_count,)),
+            dma((PACK, bead_count)), dma((PACK, bead_count)),
+            dma((bead_count,)), dma((bead_count,)),
         ],
         compiler_params=pltpu.CompilerParams(
             collective_id=0, has_side_effects=True, vmem_limit_bytes=60 * 1024 * 1024

time: 44.7 us -> 43 us (0.962)
  Pallas kernels: 42.3 us -> 40.6 us
    pallas_call x1, Pallas kernels: 42.3 us -> 40.6 us  [per_device(): pl.pallas_call(functools.partial(step_kernel, GX // grid_count, centre),...]
where the time goes in v5:
time: 43 us; the launch traced here: 42.7 us
  Pallas kernels  40.6 us (94%)
  other arithmetic  1.47 us (3%)
  between operations  0.64 us (1%)
    pallas_call x1, Pallas kernels, per_device(): pl.pallas_call(functools.partial(step_kernel, GX // grid_count, centre),...  40.6 us
    add x1, other arithmetic, per_device(): return tuple((drifted[i] + force[i][:, None, :] for i in range(2)))  1.47 us

profile of v5, /device:TPU:0, one launch (start us, length us, event | category | flops | bytes accessed | tf_op | source)
XLA Modules:
  0.0 42.7 jit_solution(8667687638261723497)
XLA Ops:
  0.6 40.6 %shard_map.176 = (f32[2,3,8,512]{3,2,1,0:T(8,128)}, f32[3,512]{1,0:T(4,128)}, f32[3,512]{1,0:T(4,128)}) custom-call(s32[4,4]{1,0:T(4,128)} %neighbours.1, f32[3,8,512]{2,1,0:T(8,128)} %positions.1, f32[3,8,512]{2,1,0:T(8,128)} %momenta.1, f32[3,8,512]{2,1,0:T(8,128)} %noise.1, f32[1,512]{1,0:T(1,128)} %bitcast.6, s32[1,512]{1,0:T(1,128)} %bitcast.7, ...), custom_call_target="tpu_custom_call" | custom-call | tf_op jit(solution)/shard_map/pallas_call | solution.py:686
  41.3 1.5 %bitcast_add_fusion = (f32[3,8,512]{2,1,0:T(8,128)}, f32[3,8,512]{2,1,0:T(8,128)}) fusion(f32[2,3,8,512]{3,2,1,0:T(8,128)} %get-tuple-element.5, f32[3,512]{1,0:T(4,128)} %get-tuple-element.7, f32[3,512]{1,0:T(4,128)} %get-tuple-element.6), kind=kLoop, calls=%fused_computation | loop fusion | flops 24576 | bytes 208896 | tf_op jit(solution)/shard_map/add | solution.py:723

commit v6 on v5

--- a/solution.py
+++ b/solution.py
@@ -151,7 +151,7 @@
     total[...] = jnp.zeros_like(total)
 
 
-def mesh_phases(fields, tables, out, track, along, total, near, filt, ready, finished):
+def mesh_phases(fields, tables, out, track, along, total, near, filt, ready, filler, filled, finished):
     domains = fields.shape[0]
     bead_count = lax.axis_size("bead")
     device = lax.axis_index("grid") * bead_count + lax.axis_index("bead")
@@ -240,6 +240,7 @@
             store(rows, each)
         return carry
 
+    filler()
     forward(0, 0)
 
     def middle(i, carry):
@@ -271,6 +272,7 @@
         return carry
 
     inverse(0, 0)
+    filled()
     near[:, cells_all:cells_all + halo, :] = near[:, 0:halo, :]
 
     half = min(8, bins)
@@ -424,31 +426,27 @@
     return jnp.where(spots == slot, 1.0, 0.0).astype(jnp.bfloat16)
 
 
-def pair_forces(weight_of, positions, momenta, kicked):
+def pair_forces(weight_of, positions, momenta, kicked, chosen):
     beads, atoms = positions.shape[1:]
-    tiles = atoms // TILE
     across = [positions[c].T for c in range(3)]
-
-    def body(t, carry):
-        where = pl.ds(pl.multiple_of(t * TILE, TILE), TILE)
-        for b in range(beads):
-            centre = [positions[c, b : b + 1, where] for c in range(3)]
-            sums = [jnp.zeros((8, TILE), jnp.float32) for _ in range(3)]
-            for m in range(tiles):
-                apart = [
-                    centre[c] - across[c][m * TILE : (m + 1) * TILE, b : b + 1] for c in range(3)
-                ]
+    spans = [slice(t * TILE, (t + 1) * TILE) for t in range(atoms // TILE)]
+    weights = [[weight_of(t, m) for m in range(len(spans))] for t in chosen]
+    for b in range(beads):
+        centres = [[positions[c, b : b + 1, spans[t]] for c in range(3)] for t in chosen]
+        sums = [[jnp.zeros((8, TILE), jnp.float32) for _ in range(3)] for _ in chosen]
+        for m, span in enumerate(spans):
+            columns = [jnp.broadcast_to(across[c][span, b : b + 1], (TILE, TILE)) for c in range(3)]
+            for i in range(len(chosen)):
+                apart = [centres[i][c] - columns[c] for c in range(3)]
                 square = apart[0] * apart[0] + apart[1] * apart[1] + apart[2] * apart[2]
                 weight = jnp.exp(square * (-1.0 / pair_range))
                 for c in range(3):
                     part = jnp.sum((weight * apart[c]).reshape(TILE // 8, 8, TILE), axis=0)
-                    sums[c] = sums[c] + weight_of(t, m) * part
+                    sums[i][c] = sums[i][c] + weights[i][m] * part
+        for i, t in enumerate(chosen):
             for c in range(3):
-                force = jnp.sum(sums[c], axis=0, keepdims=True)
-                kicked[c, b : b + 1, where] = momenta[c, b : b + 1, where] + force
-        return carry
-
-    lax.fori_loop(0, tiles, body, 0)
+                force = jnp.sum(sums[i][c], axis=0, keepdims=True)
+                kicked[c, b : b + 1, spans[t]] = momenta[c, b : b + 1, spans[t]] + force
 
 
 def step_tables(bead_total):
@@ -590,8 +588,15 @@
 
     loads[4].wait()
     loads[5].wait()
-    pair_forces(weight_of, sources.at[bead_rank, 0], own_momenta, kicks.at[bead_rank])
-    kick[0]()
+
+    def pair(chosen):
+        pair_forces(
+            weight_of, sources.at[bead_rank, 0], own_momenta, kicks.at[bead_rank], chosen
+        )
+
+    tiles = own_momenta.shape[2] // TILE
+    early = tiles - tiles // 4
+    pair(range(early))
     field[1]()
 
     def finished(pair):
@@ -605,7 +610,8 @@
             each_close(lambda step: close(step).start())
 
     mesh_phases(
-        fields, own_waves, partial, track, along, total, near, filt, loads[8].wait, finished
+        fields, own_waves, partial, track, along, total, near, filt, loads[8].wait,
+        lambda: pair(range(early, tiles)), kick[0], finished,
     )
 
     mates[place_in, bead_rank] = partial[grid_rank]

time: 43 us -> 41.1 us (0.956)
  Pallas kernels: 40.6 us -> 38.7 us
    pallas_call x1, Pallas kernels: 40.6 us -> 38.7 us  [per_device(): pl.pallas_call(functools.partial(step_kernel, GX // grid_count, centre),...]
where the time goes in v6:
time: 41.1 us; the launch traced here: 40.9 us
  Pallas kernels  38.7 us (94%)
  other arithmetic  1.47 us (4%)
  between operations  0.64 us (2%)
    pallas_call x1, Pallas kernels, per_device(): pl.pallas_call(functools.partial(step_kernel, GX // grid_count, centre),...  38.7 us
    add x1, other arithmetic, per_device(): return tuple((drifted[i] + force[i][:, None, :] for i in range(2)))  1.47 us

profile of v6, /device:TPU:0, one launch (start us, length us, event | category | flops | bytes accessed | tf_op | source)
XLA Modules:
  0.0 40.9 jit_solution(13682420291118337923)
XLA Ops:
  0.6 38.7 %shard_map.176 = (f32[2,3,8,512]{3,2,1,0:T(8,128)}, f32[3,512]{1,0:T(4,128)}, f32[3,512]{1,0:T(4,128)}) custom-call(s32[4,4]{1,0:T(4,128)} %neighbours.1, f32[3,8,512]{2,1,0:T(8,128)} %positions.1, f32[3,8,512]{2,1,0:T(8,128)} %momenta.1, f32[3,8,512]{2,1,0:T(8,128)} %noise.1, f32[1,512]{1,0:T(1,128)} %bitcast.6, s32[1,512]{1,0:T(1,128)} %bitcast.7, ...), custom_call_target="tpu_custom_call" | custom-call | tf_op jit(solution)/shard_map/pallas_call | solution.py:692
  39.4 1.5 %bitcast_add_fusion = (f32[3,8,512]{2,1,0:T(8,128)}, f32[3,8,512]{2,1,0:T(8,128)}) fusion(f32[2,3,8,512]{3,2,1,0:T(8,128)} %get-tuple-element.5, f32[3,512]{1,0:T(4,128)} %get-tuple-element.7, f32[3,512]{1,0:T(4,128)} %get-tuple-element.6), kind=kLoop, calls=%fused_computation | loop fusion | flops 24576 | bytes 208896 | tf_op jit(solution)/shard_map/add | solution.py:729

commit v7 on v6

--- a/solution.py
+++ b/solution.py
@@ -428,18 +428,19 @@
 
 def pair_forces(weight_of, positions, momenta, kicked, chosen):
     beads, atoms = positions.shape[1:]
-    across = [positions[c].T for c in range(3)]
+    halved = 1.0 / math.sqrt(pair_range)
+    across = [(positions[c] * halved).T for c in range(3)]
     spans = [slice(t * TILE, (t + 1) * TILE) for t in range(atoms // TILE)]
     weights = [[weight_of(t, m) for m in range(len(spans))] for t in chosen]
     for b in range(beads):
-        centres = [[positions[c, b : b + 1, spans[t]] for c in range(3)] for t in chosen]
+        centres = [[positions[c, b : b + 1, spans[t]] * halved for c in range(3)] for t in chosen]
         sums = [[jnp.zeros((8, TILE), jnp.float32) for _ in range(3)] for _ in chosen]
         for m, span in enumerate(spans):
             columns = [jnp.broadcast_to(across[c][span, b : b + 1], (TILE, TILE)) for c in range(3)]
             for i in range(len(chosen)):
                 apart = [centres[i][c] - columns[c] for c in range(3)]
                 square = apart[0] * apart[0] + apart[1] * apart[1] + apart[2] * apart[2]
-                weight = jnp.exp(square * (-1.0 / pair_range))
+                weight = jnp.exp(-square)
                 for c in range(3):
                     part = jnp.sum((weight * apart[c]).reshape(TILE // 8, 8, TILE), axis=0)
                     sums[i][c] = sums[i][c] + weights[i][m] * part
@@ -583,7 +584,7 @@
     def weight_of(t, m):
         total = 0.0
         for k in range(neighbours.shape[1]):
-            total += jnp.where(neighbours[t, k] == m, 0.5 * time_step * pair_strength, 0.0)
+            total += jnp.where(neighbours[t, k] == m, 0.5 * time_step * pair_strength * math.sqrt(pair_range), 0.0)
         return total
 
     loads[4].wait()

time: 41.1 us -> 41.2 us (level)
  no operation moved by 1% of the time
where the time goes in v7:
time: 41.2 us; the launch traced here: 41 us
  Pallas kernels  38.9 us (94%)
  other arithmetic  1.47 us (4%)
  between operations  0.64 us (2%)
    pallas_call x1, Pallas kernels, per_device(): pl.pallas_call(functools.partial(step_kernel, GX // grid_count, centre),...  38.9 us
    add x1, other arithmetic, per_device(): return tuple((drifted[i] + force[i][:, None, :] for i in range(2)))  1.47 us

profile of v7, /device:TPU:0, one launch (start us, length us, event | category | flops | bytes accessed | tf_op | source)
XLA Modules:
  0.0 41.0 jit_solution(4810663824388428949)
XLA Ops:
  0.6 38.9 %shard_map.176 = (f32[2,3,8,512]{3,2,1,0:T(8,128)}, f32[3,512]{1,0:T(4,128)}, f32[3,512]{1,0:T(4,128)}) custom-call(s32[4,4]{1,0:T(4,128)} %neighbours.1, f32[3,8,512]{2,1,0:T(8,128)} %positions.1, f32[3,8,512]{2,1,0:T(8,128)} %momenta.1, f32[3,8,512]{2,1,0:T(8,128)} %noise.1, f32[1,512]{1,0:T(1,128)} %bitcast.6, s32[1,512]{1,0:T(1,128)} %bitcast.7, ...), custom_call_target="tpu_custom_call" | custom-call | tf_op jit(solution)/shard_map/pallas_call | solution.py:693
  39.5 1.5 %bitcast_add_fusion = (f32[3,8,512]{2,1,0:T(8,128)}, f32[3,8,512]{2,1,0:T(8,128)}) fusion(f32[2,3,8,512]{3,2,1,0:T(8,128)} %get-tuple-element.5, f32[3,512]{1,0:T(4,128)} %get-tuple-element.7, f32[3,512]{1,0:T(4,128)} %get-tuple-element.6), kind=kLoop, calls=%fused_computation | loop fusion | flops 24576 | bytes 208896 | tf_op jit(solution)/shard_map/add | solution.py:730
